TPU v7x, 256 devices: a whole 4x4x8 slice. The times are simulated.
256 devices in a mesh: blk: 64 (over z_lo, x, y), grp: 4 (over z_hi, core).
Axes of the slice: x: 4, y: 4, z: 8 (z_hi: 2, z_lo: 4; z = z_hi * 4 + z_lo), core: 2. Of those that a mesh axis runs over, the one named last changes fastest.
Arguments:
- source_embed: bfloat16 [131072, 768], P(('blk', 'grp')), may hold values from -60 to 60
- target_embed: bfloat16 [8192, 768], P('blk'), may hold values from -18 to 18
- target_init: float32 [8192], P('blk'), may hold values from -6 to 6
- source_logw: float32 [131072], P(('blk', 'grp')), may hold values from -2 to 2
- target_logw: float32 [8192], P('blk'), may hold values from -2 to 2
Outputs:
- row_pot: float32 [131072], P(('blk', 'grp'))
- column_pot: float32 [8192], P('blk')
All inputs are finite; a program needn't handle non-finite values.
Results may differ from a plain program's by a relative error of at most 0.0003.
Values may be sent and summed in bfloat16 or wider, within the bound.
A program may use at most 128 MiB of HBM per device.

v0:
```python
import math

import jax
import jax.numpy as jnp
from jax import lax
from jax.sharding import PartitionSpec as P

D = 768
ITERS = 2


epsilon = 0.1
inverse_eps = 10.0


def row_update(cost_matrix, column_pot, row_logw):
    scores = (column_pot[None, :] - cost_matrix) * inverse_eps
    row_top = jnp.max(scores, axis=1)
    row_sum = jnp.sum(jnp.exp(scores - row_top[:, None]), axis=1)
    return epsilon * row_logw - epsilon * (row_top + jnp.log(row_sum))


def shards(source_embed, target_embed, target_init, source_logw, target_logw):
    factor = -1.0 / math.sqrt(D)
    init_full, logw_full = (
        lax.all_gather(target_init, "blk", axis=0, tiled=True),
        lax.all_gather(target_logw, "blk", axis=0, tiled=True),
    )
    block_index = lax.axis_index("blk")
    rows_target = target_embed.shape[0]
    cost_matrix = (
        lax.dot_general(
            source_embed,
            lax.all_gather(target_embed, "blk", axis=0, tiled=True),
            (((1,), (1,)), ((), ())),
            preferred_element_type=jnp.float32,
        )
        * factor
    )
    column_pot = init_full
    row_pot = jnp.zeros(source_logw.shape, jnp.float32)
    for iteration in range(ITERS):
        row_pot = row_update(cost_matrix, column_pot, source_logw)
        scores = (row_pot[:, None] - cost_matrix) * inverse_eps
        col_top = jnp.max(scores, axis=0)
        col_peak = lax.pmax(col_top.astype(jnp.bfloat16), ("blk", "grp")).astype(col_top.dtype)
        col_total = lax.psum(jnp.sum(jnp.exp(scores - col_peak[None, :]), axis=0), ("blk", "grp"))
        column_pot = epsilon * logw_full - epsilon * (col_peak + jnp.log(col_total))
    return (
        row_pot,
        lax.dynamic_slice_in_dim(column_pot, block_index * rows_target, rows_target, 0),
    )


def solution(mesh):
    in_specs = (P(("blk", "grp"), None), P("blk", None), P("blk"), P(("blk", "grp")), P("blk"))
    out_specs = (P(("blk", "grp")), P("blk"))
    return jax.shard_map(shards, mesh=mesh, in_specs=in_specs, out_specs=out_specs, check_vma=False)
```

profile of v0, /device:TPU:1, one launch (start us, length us, event | category | flops | bytes accessed | tf_op | source)
XLA Modules:
  0.0 764.0 jit_solution(6717112200024269160)
XLA Ops:
  7.2 0.0 copy-start
  7.2 0.0 all-gather.4.cloned.1.call-start
  7.2 0.7 all-gather.4.cloned.1.call-update
  7.9 164.8 %all-gather.1 = f32[64,1,128]{2,1,0:T(1,128)S(1)} all-gather(f32[1,1,128]{2,1,0:T(1,128)} %bitcast.10), channel_id=1, replica_groups=mesh['blk'=64,'grp'=4] {'blk'}, dimensions={0}, use_global_device_ids=true | all-gather | bytes 33280 | tf_op jit(solution)/shard_map/all_gather | solution.py:26
  172.7 155.8 %all-gather = f32[64,1,128]{2,1,0:T(1,128)S(1)} all-gather(f32[1,1,128]{2,1,0:T(1,128)} %bitcast.11), channel_id=1, replica_groups=mesh['blk'=64,'grp'=4] {'blk'}, dimensions={0}, use_global_device_ids=true | all-gather | bytes 33280 | tf_op jit(solution)/shard_map/all_gather | solution.py:27
  328.5 12.5 %all-gather.4.cloned.1.call-done = bf16[8192,768]{1,0:T(8,128)(2,1)} async-done(((bf16[128,768]{1,0:T(8,128)(2,1)}), bf16[8192,768]{1,0:T(8,128)(2,1)}) %all-gather.4.cloned.1.call-update) | async-done | bytes 12582928 | tf_op jit(solution)/shard_map/all_gather | solution.py:34
  341.0 0.0 copy-done
  341.0 14.9 %fusion = (f32[512]{0:T(512)S(1)}, f32[512,8192]{1,0:T(8,128)}) fusion(f32[8192]{0:T(1024)S(1)} %bitcast.8, bf16[512,768]{1,0:T(8,128)(2,1)S(1)} %copy-done, bf16[8192,768]{1,0:T(8,128)(2,1)} %all-gather.4.cloned.1.call-done), kind=kOutput, calls=%fused_computation.8 | convolution fusion | flops 6459227648 | bytes 30181376 | tf_op jit(solution)/shard_map/dot_general | solution.py:32
  355.9 0.0 copy-start.2
  355.9 9.3 %exponential_reduce_fusion.3 = f32[512]{0:T(512)S(1)} fusion(f32[512,8192]{1,0:T(8,128)} %get-tuple-element.3, f32[512]{0:T(512)S(1)} %get-tuple-element.2, f32[8192]{0:T(1024)S(1)} %bitcast.9), kind=kLoop, calls=%fused_computation.6 | loop fusion | flops 16776704 | bytes 16814080 | tf_op jit(solution)/shard_map/reduce_sum | solution.py:19
  365.3 0.0 copy-done.2
  365.3 8.4 %fusion.1 = bf16[8192]{0:T(1024)(128)(2,1)S(1)} fusion(f32[512,8192]{1,0:T(8,128)} %get-tuple-element.3, f32[512]{0:T(512)S(1)} %multiply_subtract_fusion.2), kind=kLoop, calls=%fused_computation.9 | loop fusion | flops 12574720 | bytes 16795648 | tf_op jit(solution)/shard_map/reduce_max | solution.py:45
  373.7 117.5 %pmax.14 = bf16[8192]{0:T(1024)(128)(2,1)S(1)} all-reduce(bf16[8192]{0:T(1024)(128)(2,1)S(1)} %fusion.1), channel_id=1, replica_groups=mesh['blk'=64,'grp'=4] {'blk','grp'}, use_global_device_ids=true, to_apply=%region_3.0 | all-reduce | flops 8192 | bytes 32768 | tf_op jit(solution)/shard_map/pmax | solution.py:46
  491.1 9.4 %exponential_reduce_fusion.2 = f32[8192]{0:T(1024)S(1)} fusion(f32[512,8192]{1,0:T(8,128)} %get-tuple-element.3, f32[8192]{0:T(1024)S(1)} %convert_element_type.13, f32[512]{0:T(512)S(1)} %multiply_subtract_fusion.2), kind=kLoop, calls=%fused_computation.4 | loop fusion | flops 16769024 | bytes 16844800 | tf_op jit(solution)/shard_map/reduce_sum | solution.py:47
  500.6 72.9 %psum.14 = f32[8192]{0:T(1024)S(1)} all-reduce(f32[8192]{0:T(1024)S(1)} %exponential_reduce_fusion.2), channel_id=1, replica_groups=mesh['blk'=64,'grp'=4] {'blk','grp'}, use_global_device_ids=true, to_apply=%region_5.0 | all-reduce | flops 8192 | bytes 65536 | tf_op jit(solution)/shard_map/psum | solution.py:47
  573.5 7.7 %fusion.2 = f32[512]{0:T(512)S(1)} fusion(f32[512,8192]{1,0:T(8,128)} %get-tuple-element.3, f32[8192]{0:T(1024)S(1)} %multiply_subtract_fusion), kind=kLoop, calls=%fused_computation.10 | loop fusion | flops 12582400 | bytes 16812032 | tf_op jit(solution)/shard_map/reduce_max | solution.py:18
  581.2 9.3 %exponential_reduce_fusion.1 = f32[512]{0:T(512)S(1)} fusion(f32[512,8192]{1,0:T(8,128)} %get-tuple-element.3, f32[512]{0:T(512)S(1)} %fusion.2, f32[8192]{0:T(1024)S(1)} %multiply_subtract_fusion), kind=kLoop, calls=%fused_computation.2 | loop fusion | flops 16776704 | bytes 16814080 | tf_op jit(solution)/shard_map/reduce_sum | solution.py:19
  590.6 0.0 copy-start.1
  590.6 8.4 %fusion.3 = bf16[8192]{0:T(1024)(128)(2,1)S(1)} fusion(f32[512,8192]{1,0:T(8,128)} %get-tuple-element.3, f32[512]{0:T(512)S(1)} %multiply_subtract_fusion.1), kind=kLoop, calls=%fused_computation.11 | loop fusion | flops 12574720 | bytes 16795648 | tf_op jit(solution)/shard_map/reduce_max | solution.py:45
  598.9 74.6 %pmax.15 = bf16[8192]{0:T(1024)(128)(2,1)S(1)} all-reduce(bf16[8192]{0:T(1024)(128)(2,1)S(1)} %fusion.3), channel_id=1, replica_groups=mesh['blk'=64,'grp'=4] {'blk','grp'}, use_global_device_ids=true, to_apply=%region_9.0 | all-reduce | flops 8192 | bytes 32768 | tf_op jit(solution)/shard_map/pmax | solution.py:46
  673.6 9.4 %exponential_reduce_fusion = f32[8192]{0:T(1024)S(1)} fusion(f32[512,8192]{1,0:T(8,128)} %get-tuple-element.3, f32[8192]{0:T(1024)S(1)} %convert_element_type.15, f32[512]{0:T(512)S(1)} %multiply_subtract_fusion.1), kind=kLoop, calls=%fused_computation | loop fusion | flops 16769024 | bytes 16844800 | tf_op jit(solution)/shard_map/reduce_sum | solution.py:47
  683.0 0.0 copy-done.1
  683.0 73.5 %psum.15 = f32[8192]{0:T(1024)S(1)} all-reduce(f32[8192]{0:T(1024)S(1)} %exponential_reduce_fusion), channel_id=1, replica_groups=mesh['blk'=64,'grp'=4] {'blk','grp'}, use_global_device_ids=true, to_apply=%region_11.0 | all-reduce | flops 8192 | bytes 65536 | tf_op jit(solution)/shard_map/psum | solution.py:47
  756.5 0.6 dynamic-slice_subtract_fusion
  (6 shorter events, 0.1 us)
Async XLA Ops:
  7.2 333.8 %copy-start = (bf16[512,768]{1,0:T(8,128)(2,1)S(1)}, bf16[512,768]{1,0:T(8,128)(2,1)}, u32[]{:S(2)}) copy-start(bf16[512,768]{1,0:T(8,128)(2,1)} %param.5) | copy-start | bytes 2359300
  7.2 333.8 %all-gather.4.cloned.1.call-start = ((), (), s32[]{:S(2)}) async-start(), calls=%async_computation | async-start | bytes 12779520 | tf_op jit(solution)/shard_map/all_gather | solution.py:34
  355.9 9.3 %copy-start.2 = (f32[512]{0:T(512)S(1)}, f32[512]{0:T(512)}, u32[]{:S(2)}) copy-start(f32[512]{0:T(512)} %param.8) | copy-start | bytes 6148
  590.6 92.5 %copy-start.1 = (f32[512]{0:T(512)}, f32[512]{0:T(512)S(1)}, u32[]{:S(2)}) copy-start(f32[512]{0:T(512)S(1)} %multiply_subtract_fusion.1) | copy-start | bytes 6148
Sparse Core Ops, SparseCore 0:
  9.8 331.1 all-gather.3
where the time goes:
time: 765 us; the launch traced here: 764 us
  blocking collectives  659 us (86%)
  other arithmetic  62.7 us (8%)
  matrix products  14.9 us (2%)
  between operations  14.1 us (2%)
  waiting for transfers between devices  13.2 us (2%)
    pmax x2, blocking collectives, shards(): lax.pmax(col_top.astype(jnp.bfloat16), ('blk', 'grp')).astype(col_top.dtype)  192 us
    all_gather x1, blocking collectives, shards(): lax.all_gather(target_init, 'blk', axis=0, tiled=True)  165 us
    all_gather x1, blocking collectives, shards(): lax.all_gather(target_logw, 'blk', axis=0, tiled=True)  156 us
    psum x2, blocking collectives, shards(): lax.psum(jnp.sum(jnp.exp(scores - col_peak[None, :]), axis=0), ('blk', 'g...  146 us
    reduce_sum x2, other arithmetic, shards(): jnp.sum(jnp.exp(scores - col_peak[None, :]), axis=0)  18.9 us
    reduce_sum x2, other arithmetic, row_update(): row_sum = jnp.sum(jnp.exp(scores - row_top[:, None]), axis=1)  18.7 us
    reduce_max x2, other arithmetic, shards(): col_top = jnp.max(scores, axis=0)  16.7 us
  transfers between devices with their start and end apart: 1, of which 1 were waited for; matrix products, arithmetic and copies ran while one was open for 0% of the time, Pallas kernels for 0%

commit v1 on v0

v1 whole, which is shorter than its diff:
```python
import math

import jax
import jax.numpy as jnp
from jax import lax
from jax.experimental import pallas as pl
from jax.experimental.pallas import tpu as pltpu
from jax.sharding import PartitionSpec as P

D = 768
LOG2E = math.log2(math.e)
TO2 = 10.0 * LOG2E
SCALE = TO2 / math.sqrt(D)
NX, NY, NZ = 4, 4, 8
R = 4
MESH = pl.DeviceIdType.MESH
ORDERS = (("x", "y", "z"), ("y", "z", "x"), ("z", "x", "y"))


def lse2(stack):
    top = jnp.max(stack, axis=0)
    return top + jnp.log2(jnp.sum(jnp.exp2(stack - top[None]), axis=0))


def rem4(v):
    return lax.rem(v, 4)


def kernel(
    src_in, tgt_in, init_in, slogw_in, tlogw_in, row_out, col_out,
    src, tgt, aux, cost, grep, gsend, gbuf, mrow, srow, frep, wrow, lrow, lget, frow,
    lsend, abuf, zsend, bbuf, fbuf, hbuf,
    send, recv, loc,
):
    b, g = lax.axis_index("blk"), lax.axis_index("grp")
    core, zh = rem4(g) % 2, lax.div(g, 2)
    zl, x, y = lax.div(b, 16), rem4(lax.div(b, 4)), rem4(b)
    z = zh * 4 + zl
    me = {"x": x, "y": y, "z": zl}

    def dev(px, py, pz, pc):
        return (rem4(pz) * 16 + px * 4 + py, lax.div(pz, 4) * 2 + pc)

    def step(dim, by):
        if dim == "x":
            return dev(rem4(x + by + NX), y, z, core)
        if dim == "y":
            return dev(x, rem4(y + by + NY), z, core)
        return dev(x, y, lax.rem(z + by + NZ, NZ), core)

    partner = dev(x, y, z, 1 - core)
    plane = [(dx, dy, dev(rem4(x + dx), rem4(y + dy), z, core)) for dx in range(4) for dy in range(4)][1:]
    line = [(dz, dev(x, y, lax.rem(z + dz, NZ), core)) for dz in range(1, NZ)]
    across = [(dz, dev(x, y, lax.rem(z + dz, NZ), 1 - core)) for dz in range(NZ)]

    barrier = pltpu.get_barrier_semaphore()
    peers = [p[-1] for p in plane] + [p[-1] for p in line] + [p[-1] for p in across]
    for peer in peers:
        pl.semaphore_signal(barrier, inc=1, device_id=peer, device_id_type=MESH)

    half = pl.multiple_of(core * 64, 64)
    rows_at = pl.multiple_of(core * 512, 512)
    locals_ = [pltpu.make_async_copy(src_in, src.at[pl.ds(rows_at, 512), :], loc.at[3])]
    for t, (d0, d1, d2) in enumerate(ORDERS):
        locals_.append(
            pltpu.make_async_copy(
                tgt_in.at[pl.ds(half, 64), pl.ds(256 * t, 256)],
                tgt.at[t, me[d2], me[d1], me[d0]],
                loc.at[t],
            )
        )
    for copy in locals_:
        copy.start()
    aux[zl, y, x] = jnp.concatenate([init_in[...], tlogw_in[...]], axis=0)
    wrow[core] = slogw_in[...]

    count = [0]
    started = []

    def remote(src_ref, dst_ref, to, slot=None):
        if slot is None:
            slot = count[0]
            count[0] += 1
        return pltpu.make_async_remote_copy(
            src_ref=src_ref, dst_ref=dst_ref, send_sem=send.at[slot], recv_sem=recv.at[slot],
            device_id=to, device_id_type=MESH,
        )

    def go(copy):
        copy.start()
        started.append(copy)

    def drop(copy):
        started[:] = [c for c in started if c is not copy]

    class Ring:
        def __init__(self, dim, unit, low=None, high=None):
            self.dim, self.unit = dim, unit
            self.low, self.high = low or unit, high
            self.base = count[0]
            count[0] += 4
            c = me[dim]
            self.c, self.prev, self.next, self.far = c, rem4(c + 3), rem4(c + 1), rem4(c + 2)

        def begin(self):
            u = self.unit(self.c)
            go(remote(u, u, step(self.dim, 1), self.base))
            go(remote(u, u, step(self.dim, -1), self.base + 1))

        def mid(self):
            u = self.unit(self.prev)
            remote(u, u, step(self.dim, 1), self.base).wait_recv()
            v = self.low(self.prev)
            go(remote(v, v, step(self.dim, 1), self.base + 2))
            u = self.unit(self.next)
            remote(u, u, step(self.dim, -1), self.base + 1).wait_recv()
            if self.high is not None:
                v = self.high(self.next)
                go(remote(v, v, step(self.dim, -1), self.base + 3))

        def end(self):
            v = self.low(self.far)
            remote(v, v, step(self.dim, 1), self.base + 2).wait_recv()
            if self.high is not None:
                v = self.high(self.far)
                remote(v, v, step(self.dim, -1), self.base + 3).wait_recv()

    def rings(t):
        d0, d1, d2 = ORDERS[t]
        c1, c2 = me[d1], me[d2]
        one = Ring(
            d0,
            lambda i: tgt.at[t, c2, c1, i],
            lambda i: tgt.at[t, c2, c1, i, pl.ds(0, 32), :],
            lambda i: tgt.at[t, c2, c1, i, pl.ds(32, 32), :],
        )
        two = Ring(
            d1,
            lambda i: tgt.at[t, c2, i],
            lambda i: tgt.at[t, c2, i, pl.ds(0, 2)],
            lambda i: tgt.at[t, c2, i, pl.ds(2, 2)],
        )
        three = []
        for by in (0, 3, 1, 2):
            r1 = rem4(c1 + by)
            three.append(
                Ring(
                    d2,
                    lambda i, r1=r1: tgt.at[t, i, r1],
                    lambda i, r1=r1: tgt.at[t, i, r1, pl.ds(0, 2)],
                    lambda i, r1=r1: tgt.at[t, i, r1, pl.ds(2, 2)],
                )
            )
        return one, two, three

    all_rings = [rings(t) for t in range(3)]
    aux_rings = [
        Ring("x", lambda i: aux.at[zl, y, i]),
        Ring("y", lambda i: aux.at[zl, i]),
        Ring("z", lambda i: aux.at[i]),
    ]

    for copy in locals_[1:]:
        copy.wait()
    pl.semaphore_wait(barrier, len(peers))

    for one, _, _ in all_rings:
        one.begin()
    aux_rings[0].begin()
    swap_w = remote(wrow.at[core], wrow.at[core], partner)
    go(swap_w)
    locals_[0].wait()
    mine = src.at[pl.ds(rows_at, 512), :]
    swap_src = remote(mine, mine, partner)
    go(swap_src)
    swap_slot = count[0] - 1

    for one, _, _ in all_rings:
        one.mid()
    aux_rings[0].mid()
    for one, two, three in all_rings:
        one.end()
        two.begin()
        three[0].begin()
    aux_rings[0].end()
    aux_rings[1].begin()
    for _, two, three in all_rings:
        two.mid()
        three[1].begin()
        three[2].begin()
    aux_rings[1].mid()
    for _, two, three in all_rings:
        two.end()
        three[3].begin()
    aux_rings[1].end()
    aux_rings[2].begin()

    @pl.loop(0, 16)
    def _(i):
        cost[i] = jnp.zeros((1024, 256), jnp.float32)

    other = src.at[pl.ds(pl.multiple_of(512 - core * 512, 512), 512), :]
    remote(other, other, partner, swap_slot).wait_recv()
    remote(wrow.at[1 - core], wrow.at[1 - core], partner, swap_slot - 1).wait_recv()

    def multiply(t, gx, gy):
        if t == 0:
            rhs = tgt[0, :, gy, gx]
        elif t == 1:
            rhs = tgt[1, gx, :, gy]
        else:
            rhs = tgt[2, gy, gx]
        rhs = rhs.reshape(256, 256)
        cost[gx * 4 + gy] += SCALE * lax.dot_general(
            src[:, 256 * t : 256 * t + 256], rhs, (((1,), (1,)), ((), ())),
            preferred_element_type=jnp.float32,
        )

    @pl.loop(0, 4)
    def _(i):
        multiply(1, x, i)
        multiply(2, i, y)

    for k in range(4):
        for _, _, three in all_rings:
            three[k].mid()
    aux_rings[2].mid()

    @pl.loop(0, 4)
    def _(i):
        for by in (1, 3):
            multiply(1, rem4(x + by), i)
            multiply(2, i, rem4(y + by))

    for k in range(4):
        for _, _, three in all_rings:
            three[k].end()
    aux_rings[2].end()

    @pl.loop(0, 4)
    def _(i):
        multiply(1, rem4(x + 2), i)
        multiply(2, i, rem4(y + 2))

    @pl.loop(0, 16)
    def _(i):
        multiply(0, lax.div(i, 4), rem4(i))

    lanes = lax.broadcasted_iota(jnp.int32, (1, 128), 1)
    low_half = lanes < 64

    def pair(first, second):
        a = jnp.where(low_half, first, pltpu.roll(second, 64, 1))
        c = jnp.where(low_half, pltpu.roll(first, 64, 1), second)
        return jnp.where(core == 0, a, c)

    for gx in range(4):
        for gy in range(4):
            for h in range(2):
                v = pair(aux[2 * h, gy, gx, 0:1, :], aux[2 * h + 1, gy, gx, 0:1, :])
                gbuf[gx * 4 + gy, h : h + 1, :] = v * TO2
    own_w = [
        LOG2E * pair(aux[2 * h, y, x, 1:2, :], aux[2 * h + 1, y, x, 1:2, :]) for h in range(2)
    ]
    own_w = jnp.concatenate(own_w, axis=0)

    eye = lax.broadcasted_iota(jnp.int32, (128, 128), 0) == lax.broadcasted_iota(jnp.int32, (128, 128), 1)

    def row_pass():
        for i in range(16):
            for h in range(2):
                grep[2 * i + h] = jnp.broadcast_to(gbuf[i, h : h + 1, :], (8, 128))

        @pl.loop(0, 128)
        def _(i):
            r = pl.ds(pl.multiple_of(i * 8, 8), 8)
            parts = []
            for j in range(16):
                for h in range(2):
                    parts.append(cost[j, r, 128 * h : 128 * h + 128] + grep[2 * j + h])
            stack = jnp.stack(parts)
            top = jnp.max(stack, axis=0)
            mrow[r, :] = top
            srow[r, :] = jnp.sum(jnp.exp2(stack - top[None]), axis=0)

        for q in range(8):
            r = slice(128 * q, 128 * q + 128)
            m = mrow[r, :]
            top = jnp.max(m, axis=1, keepdims=True)
            total = jnp.sum(srow[r, :] * jnp.exp2(m - top), axis=1, keepdims=True)
            value = jnp.broadcast_to(top + jnp.log2(total), (128, 128))
            lrow[q // 4, q % 4 : q % 4 + 1, :] = jnp.sum(jnp.where(eye, value, 0.0), axis=0, keepdims=True)

    def row_swap(it):
        swap = remote(lrow, lget.at[it], partner)
        go(swap)
        swap.wait_recv()
        swap.wait_send()
        drop(swap)
        a, c = lrow[...], lget[it]
        top = jnp.maximum(a, c)
        both = top + jnp.log2(jnp.exp2(a - top) + jnp.exp2(c - top))
        frow[...] = LOG2E * wrow[...] - both
        for q in range(8):
            line_ = jnp.broadcast_to(frow[q // 4, q % 4 : q % 4 + 1, :], (128, 128))
            col = jnp.sum(jnp.where(eye, line_, 0.0), axis=1, keepdims=True)
            frep[128 * q : 128 * q + 128, :] = jnp.broadcast_to(col, (128, 128))

    def col_pass():
        @pl.loop(0, 16)
        def _(i):
            for h in range(2):
                top = total = None
                for q in range(8):
                    r = slice(128 * q, 128 * q + 128)
                    v = cost[i, r, 128 * h : 128 * h + 128] + frep[r, :]
                    v = v.reshape(16, 8, 128)
                    new = jnp.max(v, axis=0)
                    if top is not None:
                        new = jnp.maximum(top, new)
                    part = jnp.sum(jnp.exp2(v - new[None]), axis=0)
                    total = part if top is None else total * jnp.exp2(top - new) + part
                    top = new
                peak = jnp.max(top, axis=0, keepdims=True)
                mass = jnp.sum(total * jnp.exp2(top - peak), axis=0, keepdims=True)
                lsend[i, h : h + 1, :] = peak + jnp.log2(mass)

    def plane_reduce(it):
        waits = []
        for k, (dx, dy, peer) in enumerate(plane):
            dst = rem4(x + dx) * 4 + rem4(y + dy)
            copy = remote(lsend.at[dst], abuf.at[it, k + 1], peer)
            go(copy)
            waits.append(copy)
        abuf[it, 0] = lsend[x * 4 + y]
        for copy in waits:
            copy.wait_recv()
            copy.wait_send()
            drop(copy)
        return lse2(abuf[it])

    row_pass()
    row_swap(0)
    col_pass()
    zsend[0] = plane_reduce(0)
    waits = []
    for dz, peer in line:
        copy = remote(zsend.at[0], bbuf.at[dz], peer)
        go(copy)
        waits.append(copy)
    bbuf[0] = zsend[0]
    for copy in waits:
        copy.wait_recv()
    gsend[...] = own_w - lse2(bbuf[...])
    gbuf[x * 4 + y] = gsend[...]
    waits = []
    for dx, dy, peer in plane:
        copy = remote(gsend, gbuf.at[x * 4 + y], peer)
        go(copy)
        waits.append((dx, dy, copy, count[0] - 1))
    for dx, dy, copy, slot in waits:
        at = gbuf.at[rem4(x + 4 - dx) * 4 + rem4(y + 4 - dy)]
        remote(at, at, partner, slot).wait_recv()

    row_pass()
    row_swap(1)
    row_out[...] = frow[core] * (1.0 / TO2)
    col_pass()
    zsend[1] = plane_reduce(1)
    waits = []
    for dz, peer in line:
        copy = remote(zsend.at[1], fbuf.at[0, dz], peer)
        go(copy)
        waits.append(copy)
    for dz, peer in across:
        copy = remote(zsend.at[1], fbuf.at[1, dz], peer)
        go(copy)
        waits.append(copy)
    fbuf[0, 0] = zsend[1]
    for copy in waits:
        copy.wait_recv()
    hbuf[core] = lse2(fbuf[0])
    hbuf[1 - core] = lse2(fbuf[1])
    at = pl.ds(lax.div(zl, 2), 1)
    first, second = hbuf[0, at, :], hbuf[1, at, :]
    even = jnp.where(low_half, first, pltpu.roll(second, 64, 1))
    odd = jnp.where(low_half, pltpu.roll(first, 64, 1), second)
    total = jnp.where(rem4(zl) % 2 == 0, even, odd)
    col_out[...] = 0.1 * tlogw_in[...] - (1.0 / TO2) * total

    for copy in started:
        copy.wait_send()


N_SEM = 72 + 12 + 2 + 2 + 30 + 7 + 15 + 15


def shards(source_embed, target_embed, target_init, source_logw, target_logw):
    f32, bf16 = jnp.float32, jnp.bfloat16
    vmem = pl.BlockSpec(memory_space=pltpu.VMEM)
    hbm = pl.BlockSpec(memory_space=pl.ANY)
    row, col = pl.pallas_call(
        kernel,
        out_shape=(jax.ShapeDtypeStruct((4, 128), f32), jax.ShapeDtypeStruct((1, 128), f32)),
        in_specs=[hbm, hbm, vmem, vmem, vmem],
        out_specs=(vmem, vmem),
        scratch_shapes=[
            pltpu.VMEM((1024, D), bf16),
            pltpu.VMEM((3, R, R, R, 64, 256), bf16),
            pltpu.VMEM((R, R, R, 2, 128), f32),
            pltpu.VMEM((16, 1024, 256), f32),
            pltpu.VMEM((32, 8, 128), f32),
            pltpu.VMEM((2, 128), f32),
            pltpu.VMEM((16, 2, 128), f32),
            pltpu.VMEM((1024, 128), f32),
            pltpu.VMEM((1024, 128), f32),
            pltpu.VMEM((1024, 128), f32),
            pltpu.VMEM((2, 4, 128), f32),
            pltpu.VMEM((2, 4, 128), f32),
            pltpu.VMEM((2, 2, 4, 128), f32),
            pltpu.VMEM((2, 4, 128), f32),
            pltpu.VMEM((16, 2, 128), f32),
            pltpu.VMEM((2, 16, 2, 128), f32),
            pltpu.VMEM((2, 2, 128), f32),
            pltpu.VMEM((8, 2, 128), f32),
            pltpu.VMEM((2, 8, 2, 128), f32),
            pltpu.VMEM((2, 2, 128), f32),
            pltpu.SemaphoreType.DMA((N_SEM,)),
            pltpu.SemaphoreType.DMA((N_SEM,)),
            pltpu.SemaphoreType.DMA((4,)),
        ],
        compiler_params=pltpu.CompilerParams(
            collective_id=0, has_side_effects=True, vmem_limit_bytes=60 * 2**20
        ),
    )(
        source_embed, target_embed, target_init.reshape(1, 128),
        source_logw.reshape(4, 128), target_logw.reshape(1, 128),
    )
    return row.reshape(512), col.reshape(128)


def solution(mesh):
    in_specs = (P(("blk", "grp"), None), P("blk", None), P("blk"), P(("blk", "grp")), P("blk"))
    out_specs = (P(("blk", "grp")), P("blk"))
    return jax.shard_map(shards, mesh=mesh, in_specs=in_specs, out_specs=out_specs, check_vma=False)
```

time: 765 us -> 107 us (0.14)
  blocking collectives: 659 us -> 0 us
  Pallas kernels: 0 us -> 104 us
  other arithmetic: 62.7 us -> 0 us
  matrix products: 14.9 us -> 0 us
  between operations: 14.1 us -> 0.65 us
  waiting for transfers between devices: 13.2 us -> 0 us
    all_gather x2 -> x0, blocking collectives: 321 us -> none  [the longest x1 165 us: shards(): lax.all_gather(target_init, 'blk', axis=0, tiled=True)]
    pmax x2 -> x0, blocking collectives: 192 us -> none  [shards(): lax.pmax(col_top.astype(jnp.bfloat16), ('blk', 'grp')).astype(col_top.dtype)]
    psum x2 -> x0, blocking collectives: 146 us -> none  [shards(): lax.psum(jnp.sum(jnp.exp(scores - col_peak[None, :]), axis=0), ('blk', 'g...]
    pallas_call x0 -> x1, Pallas kernels: none -> 104 us  [shards(): pl.pallas_call(kernel, out_shape=(jax.ShapeDtypeStruct((4, 128), f32), ja...]
    reduce_sum x4 -> x0, other arithmetic: 37.5 us -> none  [the longest x2 18.9 us: shards(): jnp.sum(jnp.exp(scores - col_peak[None, :]), axis=0)]
    reduce_max x3 -> x0, other arithmetic: 24.4 us -> none  [the longest x2 16.7 us: shards(): col_top = jnp.max(scores, axis=0)]
    dot_general x1 -> x0, matrix products: 14.9 us -> none  [shards(): lax.dot_general(source_embed, lax.all_gather(target_embed, 'blk', axis=0,...]
    all_gather x1 -> x0, waiting for transfers between devices: 12.5 us -> none  [shards(): lax.all_gather(target_embed, 'blk', axis=0, tiled=True)]
  transfers between devices with their start and end apart: 1 -> 0, of which waited for: 1 -> 0; matrix products, arithmetic and copies ran while one was open for 0% -> 0% of each run, Pallas kernels for 0% -> 0%
where the time goes in v1:
time: 107 us
  Pallas kernels  104 us (97%)
  local copies, waits for them, and re-layouts  1.8 us (2%)
    pallas_call x1, Pallas kernels, shards(): pl.pallas_call(kernel, out_shape=(jax.ShapeDtypeStruct((4, 128), f32), ja...  104 us

profile of v1, /device:TPU:1, one launch (start us, length us, event | category | flops | bytes accessed | tf_op | source)
XLA Modules:
  0.0 106.6 jit_solution(13769353542895662116)
XLA Ops:
  0.6 104.1 %shard_map.68 = (f32[4,128]{1,0:T(4,128)}, f32[1,128]{1,0:T(1,128)}) custom-call(bf16[512,768]{1,0:T(8,128)(2,1)} %src_in.1, bf16[128,768]{1,0:T(8,128)(2,1)} %tgt_in.1, f32[1,128]{1,0:T(1,128)} %bitcast.7, f32[4,128]{1,0:T(4,128)} %bitcast.5, f32[1,128]{1,0:T(1,128)} %bitcast.8), custom_call_target="tpu_custom_call" | custom-call | tf_op jit(solution)/shard_map/pallas_call | solution.py:402
  104.8 0.0 copy-start
  104.8 0.7 copy-done
  105.5 0.0 copy-start.1
  105.5 0.6 copy.9
  106.0 0.1 copy-done.1
  106.1 0.5 copy.10
Async XLA Ops:
  104.8 0.7 copy-start
  105.5 0.6 copy-start.1

commit v2 on v1

--- a/solution.py
+++ b/solution.py
@@ -14,6 +14,7 @@
 NX, NY, NZ = 4, 4, 8
 R = 4
 MESH = pl.DeviceIdType.MESH
+FAR_FIRST = (2, 1, 3, 0)
 ORDERS = (("x", "y", "z"), ("y", "z", "x"), ("z", "x", "y"))
 
 
@@ -30,7 +31,7 @@
     src_in, tgt_in, init_in, slogw_in, tlogw_in, row_out, col_out,
     src, tgt, aux, cost, grep, gsend, gbuf, mrow, srow, frep, wrow, lrow, lget, frow,
     lsend, abuf, zsend, bbuf, fbuf, hbuf,
-    send, recv, loc,
+    send, recv, loc, token,
 ):
     b, g = lax.axis_index("blk"), lax.axis_index("grp")
     core, zh = rem4(g) % 2, lax.div(g, 2)
@@ -49,12 +50,12 @@
         return dev(x, y, lax.rem(z + by + NZ, NZ), core)
 
     partner = dev(x, y, z, 1 - core)
-    plane = [(dx, dy, dev(rem4(x + dx), rem4(y + dy), z, core)) for dx in range(4) for dy in range(4)][1:]
+    plane = [(dx, dy, dev(rem4(x + dx), rem4(y + dy), z, core)) for dx in FAR_FIRST for dy in FAR_FIRST][:15]
     line = [(dz, dev(x, y, lax.rem(z + dz, NZ), core)) for dz in range(1, NZ)]
     across = [(dz, dev(x, y, lax.rem(z + dz, NZ), 1 - core)) for dz in range(NZ)]
 
     barrier = pltpu.get_barrier_semaphore()
-    peers = [p[-1] for p in plane] + [p[-1] for p in line] + [p[-1] for p in across]
+    peers = [step(d, by) for d in ("x", "y", "z") for by in (1, -1)] + [partner]
     for peer in peers:
         pl.semaphore_signal(barrier, inc=1, device_id=peer, device_id_type=MESH)
 
@@ -236,6 +237,8 @@
         for _, _, three in all_rings:
             three[k].end()
     aux_rings[2].end()
+    for by in (2, -2):
+        pl.semaphore_signal(token, inc=1, device_id=step("z", by), device_id_type=MESH)
 
     @pl.loop(0, 4)
     def _(i):
@@ -271,7 +274,7 @@
             for h in range(2):
                 grep[2 * i + h] = jnp.broadcast_to(gbuf[i, h : h + 1, :], (8, 128))
 
-        @pl.loop(0, 128)
+        @pl.loop(0, 128, unroll=4)
         def _(i):
             r = pl.ds(pl.multiple_of(i * 8, 8), 8)
             parts = []
@@ -285,11 +288,10 @@
 
         for q in range(8):
             r = slice(128 * q, 128 * q + 128)
-            m = mrow[r, :]
-            top = jnp.max(m, axis=1, keepdims=True)
-            total = jnp.sum(srow[r, :] * jnp.exp2(m - top), axis=1, keepdims=True)
-            value = jnp.broadcast_to(top + jnp.log2(total), (128, 128))
-            lrow[q // 4, q % 4 : q % 4 + 1, :] = jnp.sum(jnp.where(eye, value, 0.0), axis=0, keepdims=True)
+            m = mrow[r, :].T
+            top = jnp.max(m, axis=0, keepdims=True)
+            total = jnp.sum(srow[r, :].T * jnp.exp2(m - top), axis=0, keepdims=True)
+            lrow[q // 4, q % 4 : q % 4 + 1, :] = top + jnp.log2(total)
 
     def row_swap(it):
         swap = remote(lrow, lget.at[it], partner)
@@ -306,14 +308,29 @@
             col = jnp.sum(jnp.where(eye, line_, 0.0), axis=1, keepdims=True)
             frep[128 * q : 128 * q + 128, :] = jnp.broadcast_to(col, (128, 128))
 
-    def col_pass():
+    def far_first(i):
+        return jnp.where(i == 0, 2, jnp.where(i == 1, 1, jnp.where(i == 2, 3, 0)))
+
+    def col_reduce(it):
+        base = count[0]
+        count[0] += 15
+
+        def owner(i):
+            return rem4(x + far_first(lax.div(i, 4))), rem4(y + far_first(rem4(i)))
+
+        def give(i):
+            px, py = owner(i)
+            return remote(lsend.at[px * 4 + py], abuf.at[it, i], dev(px, py, z, core), base + i)
+
         @pl.loop(0, 16)
         def _(i):
+            px, py = owner(i)
+            at = px * 4 + py
             for h in range(2):
                 top = total = None
                 for q in range(8):
                     r = slice(128 * q, 128 * q + 128)
-                    v = cost[i, r, 128 * h : 128 * h + 128] + frep[r, :]
+                    v = cost[at, r, 128 * h : 128 * h + 128] + frep[r, :]
                     v = v.reshape(16, 8, 128)
                     new = jnp.max(v, axis=0)
                     if top is not None:
@@ -323,26 +340,26 @@
                     top = new
                 peak = jnp.max(top, axis=0, keepdims=True)
                 mass = jnp.sum(total * jnp.exp2(top - peak), axis=0, keepdims=True)
-                lsend[i, h : h + 1, :] = peak + jnp.log2(mass)
-
-    def plane_reduce(it):
-        waits = []
-        for k, (dx, dy, peer) in enumerate(plane):
-            dst = rem4(x + dx) * 4 + rem4(y + dy)
-            copy = remote(lsend.at[dst], abuf.at[it, k + 1], peer)
-            go(copy)
-            waits.append(copy)
-        abuf[it, 0] = lsend[x * 4 + y]
-        for copy in waits:
+                lsend[at, h : h + 1, :] = peak + jnp.log2(mass)
+
+            @pl.when(i > 0)
+            def _():
+                give(i - 1).start()
+
+        abuf[it, 15] = lsend[x * 4 + y]
+
+        @pl.loop(0, 15)
+        def _(i):
+            copy = give(i)
             copy.wait_recv()
             copy.wait_send()
-            drop(copy)
+
         return lse2(abuf[it])
 
     row_pass()
     row_swap(0)
-    col_pass()
-    zsend[0] = plane_reduce(0)
+    zsend[0] = col_reduce(0)
+    pl.semaphore_wait(token, 2)
     waits = []
     for dz, peer in line:
         copy = remote(zsend.at[0], bbuf.at[dz], peer)
@@ -365,8 +382,7 @@
     row_pass()
     row_swap(1)
     row_out[...] = frow[core] * (1.0 / TO2)
-    col_pass()
-    zsend[1] = plane_reduce(1)
+    zsend[1] = col_reduce(1)
     waits = []
     for dz, peer in line:
         copy = remote(zsend.at[1], fbuf.at[0, dz], peer)
@@ -428,6 +444,7 @@
             pltpu.SemaphoreType.DMA((N_SEM,)),
             pltpu.SemaphoreType.DMA((N_SEM,)),
             pltpu.SemaphoreType.DMA((4,)),
+            pltpu.SemaphoreType.REGULAR,
         ],
         compiler_params=pltpu.CompilerParams(
             collective_id=0, has_side_effects=True, vmem_limit_bytes=60 * 2**20

time: 107 us -> 96.4 us (0.901)
  Pallas kernels: 104 us -> 93.8 us
    pallas_call x1, Pallas kernels: 104 us -> 93.8 us  [shards(): pl.pallas_call(kernel, out_shape=(jax.ShapeDtypeStruct((4, 128), f32), ja...]
where the time goes in v2:
time: 96.4 us; the launch traced here: 96.3 us
  Pallas kernels  93.8 us (97%)
  local copies, waits for them, and re-layouts  1.8 us (2%)
    pallas_call x1, Pallas kernels, shards(): pl.pallas_call(kernel, out_shape=(jax.ShapeDtypeStruct((4, 128), f32), ja...  93.8 us

profile of v2, /device:TPU:1, one launch (start us, length us, event | category | flops | bytes accessed | tf_op | source)
XLA Modules:
  0.0 96.3 jit_solution(4016394643968506231)
XLA Ops:
  0.6 93.8 %shard_map.68 = (f32[4,128]{1,0:T(4,128)}, f32[1,128]{1,0:T(1,128)}) custom-call(bf16[512,768]{1,0:T(8,128)(2,1)} %src_in.1, bf16[128,768]{1,0:T(8,128)(2,1)} %tgt_in.1, f32[1,128]{1,0:T(1,128)} %bitcast.7, f32[4,128]{1,0:T(4,128)} %bitcast.5, f32[1,128]{1,0:T(1,128)} %bitcast.8), custom_call_target="tpu_custom_call" | custom-call | tf_op jit(solution)/shard_map/pallas_call | solution.py:418
  94.4 0.0 copy-start
  94.4 0.7 copy-done
  95.1 0.0 copy-start.1
  95.1 0.6 copy.9
  95.7 0.1 copy-done.1
  95.7 0.5 copy.10
Async XLA Ops:
  94.4 0.7 copy-start
  95.1 0.6 copy-start.1

commit v3 on v2

v3 whole, which is shorter than its diff:
```python
import math

import jax
import jax.numpy as jnp
from jax import lax
from jax.experimental import pallas as pl
from jax.experimental.pallas import tpu as pltpu
from jax.sharding import PartitionSpec as P

D = 768
LOG2E = math.log2(math.e)
TO2 = 10.0 * LOG2E
SCALE = TO2 / math.sqrt(D)
NZ = 8
R = 4
MESH = pl.DeviceIdType.MESH


def lse2(stack):
    top = jnp.max(stack, axis=0)
    return top + jnp.log2(jnp.sum(jnp.exp2(stack - top[None]), axis=0))


def rem4(v):
    return lax.rem(v, 4)


def kernel(
    src_in, tgt_in, init_in, slogw_in, tlogw_in, row_out, col_out,
    src, buf_a, buf_b, buf_c, aux, cost, grep, gsend, gbuf, mrow, srow, frep, wrow, lrow, lget, frow,
    ltile, lsend, abuf, zsend, bbuf, fbuf, hbuf,
    send, recv, loc, token,
):
    b, g = lax.axis_index("blk"), lax.axis_index("grp")
    core, zh = lax.rem(g, 2), lax.div(g, 2)
    zl, x, y = lax.div(b, 16), rem4(lax.div(b, 4)), rem4(b)
    z = zh * 4 + zl
    u, v = jnp.where(core == 0, x, y), jnp.where(core == 0, y, x)

    def at(du, dv, dz, pc):
        pu, pv, pz = rem4(u + du + 4), rem4(v + dv + 4), lax.rem(z + dz + NZ, NZ)
        px, py = jnp.where(core == 0, pu, pv), jnp.where(core == 0, pv, pu)
        return (rem4(pz) * 16 + px * 4 + py, lax.div(pz, 4) * 2 + pc)

    def step(dim, by):
        return at(by if dim == "u" else 0, by if dim == "v" else 0, by if dim == "z" else 0, core)

    partner = at(0, 0, 0, 1 - core)
    line = [(dz, at(0, 0, dz, core)) for dz in range(1, NZ)]
    across = [(dz, at(0, 0, dz, 1 - core)) for dz in range(NZ)]

    barrier = pltpu.get_barrier_semaphore()
    peers = [step(d, by) for d in ("u", "v", "z") for by in (1, -1)] + [partner]
    for peer in peers:
        pl.semaphore_signal(barrier, inc=1, device_id=peer, device_id_type=MESH)

    half = pl.multiple_of(core * 64, 64)
    rows_at = pl.multiple_of(core * 512, 512)
    locals_ = [
        pltpu.make_async_copy(tgt_in.at[pl.ds(half, 32), :], buf_a.at[0, 0, 0], loc.at[0]),
        pltpu.make_async_copy(tgt_in.at[pl.ds(half + 32, 16), :], buf_b.at[0, 0, 0], loc.at[1]),
        pltpu.make_async_copy(tgt_in.at[pl.ds(half + 48, 16), :], buf_c.at[0, 0, 0], loc.at[2]),
        pltpu.make_async_copy(src_in, src.at[pl.ds(rows_at, 512), :], loc.at[3]),
    ]
    for copy in locals_:
        copy.start()
    aux[0, 0, 0] = jnp.concatenate([init_in[...], tlogw_in[...]], axis=0)
    wrow[core] = slogw_in[...]

    count = [0]
    started = []

    def remote(src_ref, dst_ref, to, slot=None):
        if slot is None:
            slot = count[0]
            count[0] += 1
        return pltpu.make_async_remote_copy(
            src_ref=src_ref, dst_ref=dst_ref, send_sem=send.at[slot], recv_sem=recv.at[slot],
            device_id=to, device_id_type=MESH,
        )

    def go(copy):
        copy.start()
        started.append(copy)

    def drop(copy):
        started[:] = [c for c in started if c is not copy]

    class Ring:
        def __init__(self, dim, unit, low=None, high=None):
            self.dim, self.unit = dim, unit
            self.low, self.high = low or unit, high
            self.base = count[0]
            count[0] += 4
            self.up, self.down = step(dim, 1), step(dim, -1)

        def begin(self):
            go(remote(self.unit(0), self.unit(1), self.up, self.base))
            go(remote(self.unit(0), self.unit(2), self.down, self.base + 1))

        def mid(self):
            remote(self.unit(1), self.unit(1), self.up, self.base).wait_recv()
            go(remote(self.low(1), self.low(3), self.up, self.base + 2))
            remote(self.unit(2), self.unit(2), self.down, self.base + 1).wait_recv()
            if self.high is not None:
                go(remote(self.high(2), self.high(3), self.down, self.base + 3))

        def end(self):
            remote(self.low(3), self.low(3), self.up, self.base + 2).wait_recv()
            if self.high is not None:
                remote(self.high(3), self.high(3), self.down, self.base + 3).wait_recv()

    left, right = pl.ds(0, 384), pl.ds(384, 384)
    every = slice(None)

    class Tree:
        def __init__(self, buf, dims):
            d0, d1, d2 = dims
            self.one = Ring(
                d0, lambda p: buf.at[0, 0, p],
                lambda p: buf.at[0, 0, p, every, left], lambda p: buf.at[0, 0, p, every, right],
            )

            def single(dim, place):
                return Ring(
                    dim, lambda p: buf.at[place(p)],
                    lambda p: buf.at[place(p) + (every, left)], lambda p: buf.at[place(p) + (every, right)],
                )

            both = pl.ds(1, 2)
            self.two = [
                single(d1, lambda p: (0, p, 0)),
                Ring(d1, lambda p: buf.at[0, p, both], lambda p: buf.at[0, p, 1], lambda p: buf.at[0, p, 2]),
                single(d1, lambda p: (0, p, 3)),
            ]
            self.own = [
                single(d2, lambda p: (p, 0, 0)),
                Ring(d2, lambda p: buf.at[p, 0, both], lambda p: buf.at[p, 0, 1], lambda p: buf.at[p, 0, 2]),
                single(d2, lambda p: (p, 0, 3)),
            ]
            self.near = [
                Ring(d2, lambda p, k=k: buf.at[p, both, k], lambda p, k=k: buf.at[p, 1, k], lambda p, k=k: buf.at[p, 2, k])
                for k in (0, both, 3)
            ]
            self.far = Ring(
                d2, lambda p: buf.at[p, 3], lambda p: buf.at[p, 3, pl.ds(0, 2)], lambda p: buf.at[p, 3, pl.ds(2, 2)]
            )

    trees = [Tree(buf_a, ("v", "z", "u")), Tree(buf_b, ("u", "z", "v")), Tree(buf_c, ("u", "v", "z"))]
    aux_rings = [
        Ring("u", lambda p: aux.at[0, 0, p]),
        Ring("v", lambda p: aux.at[0, p]),
        Ring("z", lambda p: aux.at[p]),
    ]

    for copy in locals_[:3]:
        copy.wait()
    pl.semaphore_wait(barrier, len(peers))

    trees[0].one.begin()
    trees[1].one.begin()
    trees[2].one.begin()
    aux_rings[0].begin()
    trees[0].two[0].begin()
    trees[1].two[0].begin()
    trees[2].two[0].begin()
    trees[0].own[0].begin()
    trees[1].own[0].begin()
    trees[2].own[0].begin()
    swap_slot = count[0]
    go(remote(wrow.at[core], wrow.at[core], partner))
    locals_[3].wait()
    mine = src.at[pl.ds(rows_at, 512), :]
    go(remote(mine, mine, partner))
    trees[0].one.mid()
    trees[0].two[1].begin()
    trees[0].own[1].begin()
    trees[1].one.mid()
    trees[1].two[1].begin()
    trees[1].own[1].begin()
    trees[2].one.mid()
    trees[2].two[1].begin()
    aux_rings[0].mid()
    trees[0].two[0].mid()
    trees[0].near[0].begin()
    trees[1].two[0].mid()
    trees[1].near[0].begin()
    trees[2].two[0].mid()
    trees[2].near[0].begin()
    trees[0].one.end()
    trees[0].two[2].begin()
    trees[0].own[2].begin()
    trees[1].one.end()
    trees[1].two[2].begin()
    trees[1].own[2].begin()
    trees[2].one.end()
    trees[2].two[2].begin()
    aux_rings[0].end()
    aux_rings[1].begin()
    trees[2].own[1].begin()
    trees[0].two[1].mid()
    trees[0].near[1].begin()
    trees[1].two[1].mid()
    trees[1].near[1].begin()
    trees[2].two[1].mid()
    trees[2].near[1].begin()
    aux_rings[1].mid()
    trees[0].two[2].mid()
    trees[0].near[2].begin()
    trees[1].two[2].mid()
    trees[1].near[2].begin()
    trees[2].two[2].mid()
    trees[2].near[2].begin()
    trees[2].own[2].begin()
    aux_rings[1].end()
    aux_rings[2].begin()
    trees[0].own[0].mid()
    trees[1].own[0].mid()
    trees[2].own[0].mid()
    trees[0].two[0].end()
    trees[0].two[1].end()
    trees[0].two[2].end()
    trees[0].far.begin()
    trees[1].two[0].end()
    trees[1].two[1].end()
    trees[1].two[2].end()
    trees[1].far.begin()
    trees[2].two[0].end()
    trees[2].two[1].end()
    trees[2].two[2].end()
    trees[2].far.begin()
    trees[0].own[1].mid()
    trees[1].own[1].mid()
    trees[2].own[1].mid()
    trees[0].own[2].mid()
    trees[1].own[2].mid()
    trees[2].own[2].mid()
    aux_rings[2].mid()

    other = src.at[pl.ds(pl.multiple_of(512 - core * 512, 512), 512), :]
    remote(wrow.at[1 - core], wrow.at[1 - core], partner, swap_slot).wait_recv()
    remote(other, other, partner, swap_slot + 1).wait_recv()

    zplace = []
    for k in range(4):
        r = rem4(k - zl + 4)
        zplace.append(jnp.where(r == 0, 0, jnp.where(r == 3, 1, jnp.where(r == 1, 2, 3))))

    def multiply(pieces, tile):
        rhs = jnp.concatenate(pieces, axis=0)
        out = SCALE * lax.dot_general(
            src[...], rhs, (((1,), (1,)), ((), ())), preferred_element_type=jnp.float32
        )
        cost[tile] = out[:, :128]
        cost[tile + 1] = out[:, 128:]

    def multiply_a(pu, pair):
        multiply([buf_a[pu, zp, pair * 2 + k] for k in range(2) for zp in zplace], pu * 4 + pair * 2)

    def multiply_b(pv):
        multiply([buf_b[pv, zp, pu] for pu in range(4) for zp in zplace], 16 + pv * 2)

    def multiply_c(pv):
        multiply([buf_c[zp, pv, pu] for pu in range(4) for zp in zplace], 24 + pv * 2)

    trees[0].near[0].mid()
    trees[1].near[0].mid()
    trees[2].near[0].mid()

    multiply_a(0, 0)
    trees[0].near[1].mid()
    trees[1].near[1].mid()
    trees[2].near[1].mid()

    multiply_a(0, 1)
    trees[0].near[2].mid()
    trees[1].near[2].mid()
    trees[2].near[2].mid()

    multiply_b(0)
    trees[0].far.mid()
    trees[1].far.mid()
    trees[2].far.mid()
    aux_rings[2].end()

    @pl.loop(0, 4)
    def _(i):
        multiply_a(1 + lax.div(i, 2), lax.rem(i, 2))

    @pl.loop(1, 3)
    def _(i):
        multiply_b(i)

    lanes = lax.broadcasted_iota(jnp.int32, (1, 128), 1)
    low_half = lanes < 64
    z_of_first = lax.div(lanes, 32)
    z_of_second = lax.div(lax.rem(lanes, 64), 16)

    def group_of(blocks):
        first = second = jnp.zeros((1, 128), jnp.float32)
        for k, block in enumerate(blocks):
            w = jnp.where(core == 0, block, pltpu.roll(block, 64, 1))
            first = jnp.where(z_of_first == k, pltpu.roll(w, (k * 32) % 128, 1), first)
            w_low = pltpu.roll(w, (k * 16 - 32) % 128, 1)
            w_high = pltpu.roll(w, (k * 16 + 16) % 128, 1)
            second = jnp.where(z_of_second == k, jnp.where(low_half, w_low, w_high), second)
        return jnp.concatenate([first, second], axis=0)

    for pu in range(4):
        for pv in range(4):
            gbuf[pu * 4 + pv] = TO2 * group_of([aux[zp, pv, pu, 0:1, :] for zp in zplace])
    own_w = LOG2E * group_of([aux[zp, 0, 0, 1:2, :] for zp in zplace])

    eye = lax.broadcasted_iota(jnp.int32, (128, 128), 0) == lax.broadcasted_iota(jnp.int32, (128, 128), 1)

    def spread():
        for p in range(16):
            grep[p] = jnp.broadcast_to(gbuf[p, 0:1, :], (8, 128))
        for pv in range(4):
            for k in range(2):
                a, c = gbuf[8 * k + pv, 1:2, :], gbuf[8 * k + 4 + pv, 1:2, :]
                grep[16 + pv * 2 + k] = jnp.broadcast_to(jnp.where(low_half, a, pltpu.roll(c, 64, 1)), (8, 128))
                grep[24 + pv * 2 + k] = jnp.broadcast_to(jnp.where(low_half, pltpu.roll(a, 64, 1), c), (8, 128))

    def row_tiles(tiles, more=False):
        @pl.loop(0, 128, unroll=4)
        def _(i):
            r = pl.ds(pl.multiple_of(i * 8, 8), 8)
            top = total = None
            tl = list(tiles)
            if more:
                top, total = mrow[r, :], srow[r, :]
            for c in range(0, len(tl), 8):
                stack = jnp.stack([cost[t, r, :] + grep[t] for t in tl[c : c + 8]])
                new = jnp.max(stack, axis=0)
                if top is not None:
                    new = jnp.maximum(top, new)
                part = jnp.sum(jnp.exp2(stack - new[None]), axis=0)
                total = part if top is None else total * jnp.exp2(top - new) + part
                top = new
            mrow[r, :] = top
            srow[r, :] = total

    def row_lse():
        for q in range(8):
            r = slice(128 * q, 128 * q + 128)
            m = mrow[r, :].T
            top = jnp.max(m, axis=0, keepdims=True)
            total = jnp.sum(srow[r, :].T * jnp.exp2(m - top), axis=0, keepdims=True)
            lrow[q // 4, q % 4 : q % 4 + 1, :] = top + jnp.log2(total)

    def row_swap(it):
        swap = remote(lrow, lget.at[it], partner)
        go(swap)
        swap.wait_recv()
        swap.wait_send()
        drop(swap)
        a, c = lrow[...], lget[it]
        top = jnp.maximum(a, c)
        both = top + jnp.log2(jnp.exp2(a - top) + jnp.exp2(c - top))
        frow[...] = LOG2E * wrow[...] - both
        for q in range(8):
            line_ = jnp.broadcast_to(frow[q // 4, q % 4 : q % 4 + 1, :], (128, 128))
            col = jnp.sum(jnp.where(eye, line_, 0.0), axis=1, keepdims=True)
            frep[128 * q : 128 * q + 128, :] = jnp.broadcast_to(col, (128, 128))

    def offset(place):
        return jnp.where(place == 0, 0, jnp.where(place == 1, 3, jnp.where(place == 2, 1, 2)))

    def col_tile(tile):
        top = total = None
        for q in range(8):
            r = slice(128 * q, 128 * q + 128)
            w = (cost[tile, r, :] + frep[r, :]).reshape(16, 8, 128)
            new = jnp.max(w, axis=0)
            if top is not None:
                new = jnp.maximum(top, new)
            part = jnp.sum(jnp.exp2(w - new[None]), axis=0)
            total = part if top is None else total * jnp.exp2(top - new) + part
            top = new
        peak = jnp.max(top, axis=0, keepdims=True)
        mass = jnp.sum(total * jnp.exp2(top - peak), axis=0, keepdims=True)
        return peak + jnp.log2(mass)

    def col_reduce(it):
        base = count[0]
        count[0] += 16

        def give(p):
            to = at(offset(lax.div(p, 4)), offset(rem4(p)), 0, core)
            return remote(lsend.at[p], abuf.at[it, p], to, base + p)

        def places(i):
            pv, k = 3 - lax.div(i, 2), 1 - lax.rem(i, 2)
            return pv, k, 8 * k + pv, 8 * k + 4 + pv

        @pl.loop(0, 8)
        def _(i):
            pv, k, first, second = places(i)
            ltile[0] = col_tile(first)
            ltile[1] = col_tile(second)
            ltile[2] = col_tile(16 + pv * 2 + k)
            ltile[3] = col_tile(24 + pv * 2 + k)
            tb, tc = ltile[2], ltile[3]
            lsend[first, 0:1, :] = ltile[0]
            lsend[first, 1:2, :] = jnp.where(low_half, tb, pltpu.roll(tc, 64, 1))
            lsend[second, 0:1, :] = ltile[1]
            lsend[second, 1:2, :] = jnp.where(low_half, pltpu.roll(tb, 64, 1), tc)

            @pl.when(i > 0)
            def _():
                _, _, a, c = places(i - 1)
                give(c).start()
                give(a).start()

        give(4).start()
        abuf[it, 0] = lsend[0]

        @pl.loop(1, 16)
        def _(p):
            copy = give(p)
            copy.wait_recv()
            copy.wait_send()

        return lse2(abuf[it])

    early = list(range(12)) + list(range(16, 22))
    late = [j for j in range(32) if j not in early]
    spread()
    row_tiles(early)

    for t in trees:
        for ring in t.own + t.near:
            ring.end()
        t.far.end()
    for by in (2, -2):
        pl.semaphore_signal(token, inc=1, device_id=step("z", by), device_id_type=MESH)

    @pl.loop(0, 2)
    def _(i):
        multiply_a(3, i)

    multiply_b(3)

    @pl.loop(0, 4)
    def _(i):
        multiply_c(i)

    row_tiles(late, more=True)
    row_lse()
    row_swap(0)
    zsend[0] = col_reduce(0)
    pl.semaphore_wait(token, 2)
    waits = []
    for dz, peer in line:
        copy = remote(zsend.at[0], bbuf.at[dz], peer)
        go(copy)
        waits.append(copy)
    bbuf[0] = zsend[0]
    for copy in waits:
        copy.wait_recv()
    gsend[...] = own_w - lse2(bbuf[...])
    gbuf[0] = gsend[...]
    waits = []
    place_of, offset_of = (0, 2, 3, 1), (0, 3, 1, 2)
    for p in range(15, 0, -1):
        du, dv = offset_of[p // 4], offset_of[p % 4]
        there = place_of[(4 - du) % 4] * 4 + place_of[(4 - dv) % 4]
        copy = remote(gsend, gbuf.at[there], at(du, dv, 0, core))
        go(copy)
        waits.append((there, count[0] - 1))
    for there, slot in waits:
        remote(gbuf.at[there], gbuf.at[there], partner, slot).wait_recv()

    spread()
    row_tiles(range(32))
    row_lse()
    row_swap(1)
    row_out[...] = frow[core] * (1.0 / TO2)
    zsend[1] = col_reduce(1)
    waits = []
    for dz, peer in line:
        copy = remote(zsend.at[1], fbuf.at[0, dz], peer)
        go(copy)
        waits.append(copy)
    for dz, peer in across:
        copy = remote(zsend.at[1], fbuf.at[1, dz], peer)
        go(copy)
        waits.append(copy)
    fbuf[0, 0] = zsend[1]
    for copy in waits:
        copy.wait_recv()
    hbuf[core] = lse2(fbuf[0])
    hbuf[1 - core] = lse2(fbuf[1])
    total = jnp.zeros((1, 128), jnp.float32)
    within = lax.rem(lanes, 64)
    for c in range(2):
        first, second = hbuf[c, 0:1, :], hbuf[c, 1:2, :]
        out = jnp.zeros((1, 128), jnp.float32)
        for k in range(4):
            w = pltpu.roll(first, (64 * c - 32 * k) % 128, 1)
            w = jnp.where(within < 32, w, pltpu.roll(second, (64 * c + 32 - 16 * k) % 128, 1))
            w = jnp.where(within < 48, w, pltpu.roll(second, (64 * c - 16 - 16 * k) % 128, 1))
            out = jnp.where(zl == k, w, out)
        total = jnp.where(lax.div(lanes, 64) == c, out, total)
    col_out[...] = 0.1 * tlogw_in[...] - (1.0 / TO2) * total

    for copy in started:
        copy.wait_send()


N_SEM = 132 + 12 + 2 + 2 + 32 + 7 + 15 + 15


def shards(source_embed, target_embed, target_init, source_logw, target_logw):
    f32, bf16 = jnp.float32, jnp.bfloat16
    vmem = pl.BlockSpec(memory_space=pltpu.VMEM)
    hbm = pl.BlockSpec(memory_space=pl.ANY)
    row, col = pl.pallas_call(
        kernel,
        out_shape=(jax.ShapeDtypeStruct((4, 128), f32), jax.ShapeDtypeStruct((1, 128), f32)),
        in_specs=[hbm, hbm, vmem, vmem, vmem],
        out_specs=(vmem, vmem),
        scratch_shapes=[
            pltpu.VMEM((1024, D), bf16),
            pltpu.VMEM((R, R, R, 32, D), bf16),
            pltpu.VMEM((R, R, R, 16, D), bf16),
            pltpu.VMEM((R, R, R, 16, D), bf16),
            pltpu.VMEM((R, R, R, 2, 128), f32),
            pltpu.VMEM((32, 1024, 128), f32),
            pltpu.VMEM((32, 8, 128), f32),
            pltpu.VMEM((2, 128), f32),
            pltpu.VMEM((16, 2, 128), f32),
            pltpu.VMEM((1024, 128), f32),
            pltpu.VMEM((1024, 128), f32),
            pltpu.VMEM((1024, 128), f32),
            pltpu.VMEM((2, 4, 128), f32),
            pltpu.VMEM((2, 4, 128), f32),
            pltpu.VMEM((2, 2, 4, 128), f32),
            pltpu.VMEM((2, 4, 128), f32),
            pltpu.VMEM((4, 1, 128), f32),
            pltpu.VMEM((16, 2, 128), f32),
            pltpu.VMEM((2, 16, 2, 128), f32),
            pltpu.VMEM((2, 2, 128), f32),
            pltpu.VMEM((8, 2, 128), f32),
            pltpu.VMEM((2, 8, 2, 128), f32),
            pltpu.VMEM((2, 2, 128), f32),
            pltpu.SemaphoreType.DMA((N_SEM,)),
            pltpu.SemaphoreType.DMA((N_SEM,)),
            pltpu.SemaphoreType.DMA((4,)),
            pltpu.SemaphoreType.REGULAR,
        ],
        compiler_params=pltpu.CompilerParams(
            collective_id=0, has_side_effects=True, vmem_limit_bytes=60 * 2**20
        ),
    )(
        source_embed, target_embed, target_init.reshape(1, 128),
        source_logw.reshape(4, 128), target_logw.reshape(1, 128),
    )
    return row.reshape(512), col.reshape(128)


def solution(mesh):
    in_specs = (P(("blk", "grp"), None), P("blk", None), P("blk"), P(("blk", "grp")), P("blk"))
    out_specs = (P(("blk", "grp")), P("blk"))
    return jax.shard_map(shards, mesh=mesh, in_specs=in_specs, out_specs=out_specs, check_vma=False)
```

time: 96.4 us -> 89.9 us (0.933)
  Pallas kernels: 93.8 us -> 87.3 us
    pallas_call x1, Pallas kernels: 93.8 us -> 87.3 us  [shards(): pl.pallas_call(kernel, out_shape=(jax.ShapeDtypeStruct((4, 128), f32), ja...]
where the time goes in v3:
time: 89.9 us; the launch traced here: 89.7 us
  Pallas kernels  87.3 us (97%)
  local copies, waits for them, and re-layouts  1.8 us (2%)
    pallas_call x1, Pallas kernels, shards(): pl.pallas_call(kernel, out_shape=(jax.ShapeDtypeStruct((4, 128), f32), ja...  87.3 us
    unnamed x6, local copies, waits for them, and re-layouts  1.8 us

profile of v3, /device:TPU:1, one launch (start us, length us, event | category | flops | bytes accessed | tf_op | source)
XLA Modules:
  0.0 89.7 jit_solution(2428326164454419657)
XLA Ops:
  0.6 87.3 %shard_map.68 = (f32[4,128]{1,0:T(4,128)}, f32[1,128]{1,0:T(1,128)}) custom-call(bf16[512,768]{1,0:T(8,128)(2,1)} %src_in.1, bf16[128,768]{1,0:T(8,128)(2,1)} %tgt_in.1, f32[1,128]{1,0:T(1,128)} %bitcast.7, f32[4,128]{1,0:T(4,128)} %bitcast.5, f32[1,128]{1,0:T(1,128)} %bitcast.8), custom_call_target="tpu_custom_call" | custom-call | tf_op jit(solution)/shard_map/pallas_call | solution.py:519
  87.9 0.0 copy-start
  87.9 0.7 copy-done
  88.6 0.0 copy-start.1
  88.6 0.6 copy.9
  89.2 0.1 copy-done.1
  89.2 0.5 copy.10
Async XLA Ops:
  87.9 0.7 copy-start
  88.6 0.6 copy-start.1

commit v4 on v3

v4 whole, which is shorter than its diff:
```python
import math

import jax
import jax.numpy as jnp
from jax import lax
from jax.experimental import pallas as pl
from jax.experimental.pallas import tpu as pltpu
from jax.sharding import PartitionSpec as P

D = 768
LOG2E = math.log2(math.e)
TO2 = 10.0 * LOG2E
SCALE = TO2 / math.sqrt(D)
NZ = 8
R = 4
MESH = pl.DeviceIdType.MESH


def lse2(stack):
    top = jnp.max(stack, axis=0)
    return top + jnp.log2(jnp.sum(jnp.exp2(stack - top[None]), axis=0))


def rem4(v):
    return lax.rem(v, 4)


def kernel(
    src_in, tgt_in, init_in, slogw_in, tlogw_in, row_out, col_out,
    src, buf_a, buf_b, aux, cost, grep, gsend, gbuf, mrow, srow, frep, wrow, lrow, lget, frow,
    ltile, lsend, abuf, zsend, bbuf, fbuf, hbuf,
    send, recv, loc, token,
):
    b, g = lax.axis_index("blk"), lax.axis_index("grp")
    core, zh = lax.rem(g, 2), lax.div(g, 2)
    zl, x, y = lax.div(b, 16), rem4(lax.div(b, 4)), rem4(b)
    z = zh * 4 + zl
    x_in, x_out = x + 1 - 2 * lax.rem(x, 2), 3 - x

    def dev(px, py, pz, pc):
        return (rem4(pz) * 16 + px * 4 + py, lax.div(pz, 4) * 2 + pc)

    def at(out, dy, dz, pc):
        px = jnp.where(out == 1, x_out, x)
        return dev(px, rem4(y + dy + 4), lax.rem(z + dz + NZ, NZ), pc)

    def step(dim, by):
        return at(0, by if dim == "y" else 0, by if dim == "z" else 0, core)

    partner = at(0, 0, 0, 1 - core)
    mates = [partner, dev(x_in, y, z, core), dev(x_in, y, z, 1 - core)]
    opposite = at(1, 0, 0, core)
    line = [(dz, at(0, 0, dz, core)) for dz in range(1, NZ)]
    across = [(dz, at(0, 0, dz, 1 - core)) for dz in range(NZ)]

    barrier = pltpu.get_barrier_semaphore()
    peers = [step(d, by) for d in ("y", "z") for by in (1, -1)] + mates + [opposite]
    for peer in peers:
        pl.semaphore_signal(barrier, inc=1, device_id=peer, device_id_type=MESH)

    half = pl.multiple_of(core * 64, 64)
    locals_ = [
        pltpu.make_async_copy(tgt_in.at[pl.ds(half, 32), :], buf_a.at[0, 0, 0], loc.at[0]),
        pltpu.make_async_copy(tgt_in.at[pl.ds(half + 32, 32), :], buf_b.at[0, 0, 0], loc.at[1]),
        pltpu.make_async_copy(src_in, src.at[pl.ds(0, 512), :], loc.at[2]),
    ]
    for copy in locals_:
        copy.start()
    aux[0, 0, 0] = jnp.concatenate([init_in[...], tlogw_in[...]], axis=0)
    wrow[0] = slogw_in[...]

    count = [0]
    started = []

    def remote(src_ref, dst_ref, to, slot=None):
        if slot is None:
            slot = count[0]
            count[0] += 1
        return pltpu.make_async_remote_copy(
            src_ref=src_ref, dst_ref=dst_ref, send_sem=send.at[slot], recv_sem=recv.at[slot],
            device_id=to, device_id_type=MESH,
        )

    def go(copy):
        copy.start()
        started.append(copy)

    def drop(copy):
        started[:] = [c for c in started if c is not copy]

    class Ring:
        def __init__(self, dim, unit, low=None, high=None):
            self.dim, self.unit = dim, unit
            self.low, self.high = low or unit, high
            self.base = count[0]
            count[0] += 4
            self.up, self.down = step(dim, 1), step(dim, -1)

        def begin(self):
            go(remote(self.unit(0), self.unit(1), self.up, self.base))
            go(remote(self.unit(0), self.unit(2), self.down, self.base + 1))

        def mid(self):
            remote(self.unit(1), self.unit(1), self.up, self.base).wait_recv()
            go(remote(self.low(1), self.low(3), self.up, self.base + 2))
            remote(self.unit(2), self.unit(2), self.down, self.base + 1).wait_recv()
            if self.high is not None:
                go(remote(self.high(2), self.high(3), self.down, self.base + 3))

        def end(self):
            remote(self.low(3), self.low(3), self.up, self.base + 2).wait_recv()
            if self.high is not None:
                remote(self.high(3), self.high(3), self.down, self.base + 3).wait_recv()

    class Tree:
        def __init__(self, buf, d1, d2):
            top, end = pl.ds(0, 16), pl.ds(16, 16)
            self.first = remote(buf.at[0, 0, 0], buf.at[0, 0, 1], opposite)

            def single(dim, place):
                return Ring(
                    dim, lambda p: buf.at[place(p)], lambda p: buf.at[place(p) + (top,)], lambda p: buf.at[place(p) + (end,)]
                )

            self.two = [single(d1, lambda p, k=k: (0, p, k)) for k in range(2)]
            self.own = [single(d2, lambda p, k=k: (p, 0, k)) for k in range(2)]
            self.near = [
                Ring(d2, lambda p, k=k: buf.at[p, pl.ds(1, 2), k], lambda p, k=k: buf.at[p, 1, k], lambda p, k=k: buf.at[p, 2, k])
                for k in range(2)
            ]
            self.far = [single(d2, lambda p, k=k: (p, 3, k)) for k in range(2)]

    trees = [Tree(buf_a, "z", "y"), Tree(buf_b, "y", "z")]
    aux_first = remote(aux.at[0, 0, 0], aux.at[0, 0, 1], opposite)
    aux_rings = [Ring("y", lambda p: aux.at[0, p]), Ring("z", lambda p: aux.at[p])]

    def rows(slot, k):
        return src.at[pl.ds(512 * slot + 128 * k, 128), :]

    to_mate = [remote(rows(0, k), rows(2, k), mates[1]) for k in range(4)]
    to_partner = remote(src.at[pl.ds(0, 512), :], src.at[pl.ds(512, 512), :], partner)
    relay = [remote(rows(2, k), rows(3, k), partner) for k in range(4)]
    to_all = [remote(wrow.at[0], wrow.at[k + 1], mates[k]) for k in range(3)]

    for copy in locals_[:2]:
        copy.wait()
    pl.semaphore_wait(barrier, len(peers))

    for t in trees:
        go(t.first)
        t.two[0].begin()
        t.own[0].begin()
    go(aux_first)
    locals_[2].wait()
    for copy in to_mate:
        go(copy)
    go(to_partner)
    for copy in to_all:
        go(copy)

    for t in trees:
        t.first.wait_recv()
        t.two[1].begin()
        t.own[1].begin()
    aux_first.wait_recv()
    aux_rings[0].begin()
    for t in trees:
        t.two[0].mid()
        t.near[0].begin()
    aux_rings[0].mid()
    for t in trees:
        t.two[1].mid()
        t.near[1].begin()
    aux_rings[0].end()
    aux_rings[1].begin()
    for t in trees:
        t.two[0].end()
        t.far[0].begin()
    to_mate[0].wait_recv()
    go(relay[0])
    for t in trees:
        t.two[1].end()
        t.far[1].begin()
    for k in range(2):
        for t in trees:
            t.own[k].mid()
    aux_rings[1].mid()
    for copy in to_all:
        copy.wait_recv()
    to_partner.wait_recv()

    zplace = []
    for k in range(4):
        r = rem4(k - zl + 4)
        zplace.append(jnp.where(r == 0, 0, jnp.where(r == 3, 1, jnp.where(r == 1, 2, 3))))

    def multiply(h, pieces, tiles):
        r = slice(1024 * h, 1024 * h + 1024)
        out = SCALE * lax.dot_general(
            src[r, :], jnp.concatenate(pieces, axis=0), (((1,), (1,)), ((), ())), preferred_element_type=jnp.float32
        )
        cost[tiles[0], r, :] = out[:, :128]
        cost[tiles[1], r, :] = out[:, 128:]

    def multiply_a(h, pv):
        multiply(h, [buf_a[pv, zp, k] for k in range(2) for zp in zplace], (pv, 4 + pv))

    def multiply_b(h, pz):
        multiply(h, [buf_b[pz, pv, k] for k in range(2) for pv in range(4)], (8 + 2 * pz, 9 + 2 * pz))

    for t in trees:
        t.near[0].mid()
    multiply_a(0, 0)
    for t in trees:
        t.near[1].mid()
    to_mate[1].wait_recv()
    go(relay[1])
    multiply_b(0, 0)
    for k in range(2):
        for t in trees:
            t.far[k].mid()
    aux_rings[1].end()
    to_mate[2].wait_recv()
    go(relay[2])

    @pl.loop(1, 3)
    def _(i):
        multiply_a(0, i)
        multiply_b(0, i)

    to_mate[3].wait_recv()
    go(relay[3])

    lanes = lax.broadcasted_iota(jnp.int32, (1, 128), 1)
    low_half = lanes < 64
    chunk = lax.div(lanes, 32)

    def group_of(blocks):
        first = second = jnp.zeros((1, 128), jnp.float32)
        for k, block in enumerate(blocks):
            w = jnp.where(core == 0, block, pltpu.roll(block, 64, 1))
            first = jnp.where(chunk == k, pltpu.roll(w, (k * 32) % 128, 1), first)
            second = jnp.where(chunk == k, pltpu.roll(w, (k * 32 - 32) % 128, 1), second)
        return jnp.concatenate([first, second], axis=0)

    for k in range(2):
        for pv in range(4):
            gbuf[k * 4 + pv] = TO2 * group_of([aux[zp, pv, k, 0:1, :] for zp in zplace])
    own_w = LOG2E * group_of([aux[zp, 0, 0, 1:2, :] for zp in zplace])

    eye = lax.broadcasted_iota(jnp.int32, (128, 128), 0) == lax.broadcasted_iota(jnp.int32, (128, 128), 1)

    def spread():
        for p in range(8):
            grep[p] = jnp.broadcast_to(gbuf[p, 0:1, :], (8, 128))
        for n, zp in enumerate(zplace):
            for k in range(2):
                tile = jnp.zeros((1, 128), jnp.float32)
                for pv in range(4):
                    w = pltpu.roll(gbuf[k * 4 + pv, 1:2, :], (32 * pv - 32 * n) % 128, 1)
                    tile = jnp.where(chunk == pv, w, tile)
                grep[8 + zp * 2 + k] = jnp.broadcast_to(tile, (8, 128))

    def row_tiles(tiles, more=False):
        @pl.loop(0, 256, unroll=8)
        def _(i):
            r = pl.ds(pl.multiple_of(i * 8, 8), 8)
            top = total = None
            tl = list(tiles)
            if more:
                top, total = mrow[r, :], srow[r, :]
            for c in range(0, len(tl), 8):
                stack = jnp.stack([cost[t, r, :] + grep[t] for t in tl[c : c + 8]])
                new = jnp.max(stack, axis=0)
                if top is not None:
                    new = jnp.maximum(top, new)
                part = jnp.sum(jnp.exp2(stack - new[None]), axis=0)
                total = part if top is None else total * jnp.exp2(top - new) + part
                top = new
            mrow[r, :] = top
            srow[r, :] = total

    def row_lse():
        for q in range(16):
            r = slice(128 * q, 128 * q + 128)
            m = mrow[r, :].T
            top = jnp.max(m, axis=0, keepdims=True)
            total = jnp.sum(srow[r, :].T * jnp.exp2(m - top), axis=0, keepdims=True)
            lrow[q // 4, q % 4 : q % 4 + 1, :] = top + jnp.log2(total)

    def row_swap(it):
        swaps = [remote(lrow, lget.at[it, k], mates[k]) for k in range(3)]
        for copy in swaps:
            copy.start()
        for copy in swaps:
            copy.wait_recv()
            copy.wait_send()
        for slot in range(4):
            terms = [lrow[slot]] + [lget[it, k, slot ^ (k + 1)] for k in range(3)]
            frow[slot] = LOG2E * wrow[slot] - lse2(jnp.stack(terms))
        for q in range(16):
            line_ = jnp.broadcast_to(frow[q // 4, q % 4 : q % 4 + 1, :], (128, 128))
            col = jnp.sum(jnp.where(eye, line_, 0.0), axis=1, keepdims=True)
            frep[128 * q : 128 * q + 128, :] = jnp.broadcast_to(col, (128, 128))

    def offset(place):
        return jnp.where(place == 0, 0, jnp.where(place == 1, 3, jnp.where(place == 2, 1, 2)))

    def col_tile(tile):
        top = total = None
        for q in range(16):
            r = slice(128 * q, 128 * q + 128)
            w = (cost[tile, r, :] + frep[r, :]).reshape(16, 8, 128)
            new = jnp.max(w, axis=0)
            if top is not None:
                new = jnp.maximum(top, new)
            part = jnp.sum(jnp.exp2(w - new[None]), axis=0)
            total = part if top is None else total * jnp.exp2(top - new) + part
            top = new
        peak = jnp.max(top, axis=0, keepdims=True)
        mass = jnp.sum(total * jnp.exp2(top - peak), axis=0, keepdims=True)
        return peak + jnp.log2(mass)

    def col_reduce(it):
        base = count[0]
        count[0] += 8

        def give(p):
            to = at(lax.div(p, 4), offset(rem4(p)), 0, core)
            return remote(lsend.at[p], abuf.at[it, p], to, base + p)

        def group(i):
            return (1 - lax.rem(i, 2)) * 4 + 3 - lax.div(i, 2)

        @pl.loop(0, 8)
        def _(i):
            ltile[i] = col_tile(8 + i)

        for k in range(2):
            for pv in range(4):
                line_ = jnp.zeros((1, 128), jnp.float32)
                for n, zp in enumerate(zplace):
                    w = pltpu.roll(ltile[zp * 2 + k], (32 * n - 32 * pv) % 128, 1)
                    line_ = jnp.where(chunk == n, w, line_)
                lsend[k * 4 + pv, 1:2, :] = line_

        @pl.loop(0, 8)
        def _(i):
            p = group(i)
            lsend[p, 0:1, :] = col_tile(p)

            @pl.when(i > 0)
            def _():
                give(group(i - 1)).start()

        abuf[it, 0] = lsend[0]

        @pl.loop(1, 8)
        def _(p):
            copy = give(p)
            copy.wait_recv()
            copy.wait_send()

        return lse2(abuf[it])

    for copy in relay:
        copy.wait_recv()

    @pl.loop(0, 3)
    def _(i):
        multiply_a(1, i)
        multiply_b(1, i)

    for t in trees:
        for ring in t.own + t.near + t.far:
            ring.end()
    for by in (2, -2):
        pl.semaphore_signal(token, inc=1, device_id=step("z", by), device_id_type=MESH)
    for n in range(2):
        multiply_a(n, 3)
        multiply_b(n, 3)

    spread()
    row_tiles(range(16))
    row_lse()
    row_swap(0)
    zsend[0] = col_reduce(0)
    pl.semaphore_wait(token, 2)
    waits = []
    for dz, peer in line:
        copy = remote(zsend.at[0], bbuf.at[dz], peer)
        go(copy)
        waits.append(copy)
    bbuf[0] = zsend[0]
    for copy in waits:
        copy.wait_recv()
    gsend[...] = own_w - lse2(bbuf[...])
    gbuf[0] = gsend[...]
    waits = []
    place_of, offset_of = (0, 2, 3, 1), (0, 3, 1, 2)
    for p in range(7, 0, -1):
        out, dy = p // 4, offset_of[p % 4]
        there = out * 4 + place_of[(4 - dy) % 4]
        copy = remote(gsend, gbuf.at[there], at(out, dy, 0, core))
        go(copy)
        waits.append((there, count[0] - 1))
    for there, slot in waits:
        remote(gbuf.at[there], gbuf.at[there], partner, slot).wait_recv()

    spread()
    row_tiles(range(16))
    row_lse()
    row_swap(1)
    row_out[...] = frow[0] * (1.0 / TO2)
    zsend[1] = col_reduce(1)
    waits = []
    for dz, peer in line:
        copy = remote(zsend.at[1], fbuf.at[0, dz], peer)
        go(copy)
        waits.append(copy)
    for dz, peer in across:
        copy = remote(zsend.at[1], fbuf.at[1, dz], peer)
        go(copy)
        waits.append(copy)
    fbuf[0, 0] = zsend[1]
    for copy in waits:
        copy.wait_recv()
    hbuf[core] = lse2(fbuf[0])
    hbuf[1 - core] = lse2(fbuf[1])
    total = jnp.zeros((1, 128), jnp.float32)
    within = lax.rem(lanes, 64)
    for c in range(2):
        first, second = hbuf[c, 0:1, :], hbuf[c, 1:2, :]
        out = jnp.zeros((1, 128), jnp.float32)
        for k in range(4):
            w = jnp.where(
                within < 32,
                pltpu.roll(first, (64 * c - 32 * k) % 128, 1),
                pltpu.roll(second, (64 * c + 32 - 32 * k) % 128, 1),
            )
            out = jnp.where(zl == k, w, out)
        total = jnp.where(lax.div(lanes, 64) == c, out, total)
    col_out[...] = 0.1 * tlogw_in[...] - (1.0 / TO2) * total

    for copy in started:
        copy.wait_send()


N_SEM = 66 + 9 + 12 + 6 + 16 + 7 + 7 + 15


def shards(source_embed, target_embed, target_init, source_logw, target_logw):
    f32, bf16 = jnp.float32, jnp.bfloat16
    vmem = pl.BlockSpec(memory_space=pltpu.VMEM)
    hbm = pl.BlockSpec(memory_space=pl.ANY)
    row, col = pl.pallas_call(
        kernel,
        out_shape=(jax.ShapeDtypeStruct((4, 128), f32), jax.ShapeDtypeStruct((1, 128), f32)),
        in_specs=[hbm, hbm, vmem, vmem, vmem],
        out_specs=(vmem, vmem),
        scratch_shapes=[
            pltpu.VMEM((2048, D), bf16),
            pltpu.VMEM((R, R, 2, 32, D), bf16),
            pltpu.VMEM((R, R, 2, 32, D), bf16),
            pltpu.VMEM((R, R, 2, 2, 128), f32),
            pltpu.VMEM((16, 2048, 128), f32),
            pltpu.VMEM((16, 8, 128), f32),
            pltpu.VMEM((2, 128), f32),
            pltpu.VMEM((8, 2, 128), f32),
            pltpu.VMEM((2048, 128), f32),
            pltpu.VMEM((2048, 128), f32),
            pltpu.VMEM((2048, 128), f32),
            pltpu.VMEM((4, 4, 128), f32),
            pltpu.VMEM((4, 4, 128), f32),
            pltpu.VMEM((2, 3, 4, 4, 128), f32),
            pltpu.VMEM((4, 4, 128), f32),
            pltpu.VMEM((8, 1, 128), f32),
            pltpu.VMEM((8, 2, 128), f32),
            pltpu.VMEM((2, 8, 2, 128), f32),
            pltpu.VMEM((2, 2, 128), f32),
            pltpu.VMEM((8, 2, 128), f32),
            pltpu.VMEM((2, 8, 2, 128), f32),
            pltpu.VMEM((2, 2, 128), f32),
            pltpu.SemaphoreType.DMA((N_SEM,)),
            pltpu.SemaphoreType.DMA((N_SEM,)),
            pltpu.SemaphoreType.DMA((4,)),
            pltpu.SemaphoreType.REGULAR,
        ],
        compiler_params=pltpu.CompilerParams(
            collective_id=0, has_side_effects=True, vmem_limit_bytes=60 * 2**20
        ),
    )(
        source_embed, target_embed, target_init.reshape(1, 128),
        source_logw.reshape(4, 128), target_logw.reshape(1, 128),
    )
    return row.reshape(512), col.reshape(128)


def solution(mesh):
    in_specs = (P(("blk", "grp"), None), P("blk", None), P("blk"), P(("blk", "grp")), P("blk"))
    out_specs = (P(("blk", "grp")), P("blk"))
    return jax.shard_map(shards, mesh=mesh, in_specs=in_specs, out_specs=out_specs, check_vma=False)
```

time: 89.9 us -> 85.4 us (0.950)
  Pallas kernels: 87.3 us -> 82.8 us
    pallas_call x1, Pallas kernels: 87.3 us -> 82.8 us  [shards(): pl.pallas_call(kernel, out_shape=(jax.ShapeDtypeStruct((4, 128), f32), ja...]
where the time goes in v4:
time: 85.4 us; the launch traced here: 85.2 us
  Pallas kernels  82.8 us (97%)
  local copies, waits for them, and re-layouts  1.8 us (2%)
    pallas_call x1, Pallas kernels, shards(): pl.pallas_call(kernel, out_shape=(jax.ShapeDtypeStruct((4, 128), f32), ja...  82.8 us
    unnamed x6, local copies, waits for them, and re-layouts  1.8 us

profile of v4, /device:TPU:1, one launch (start us, length us, event | category | flops | bytes accessed | tf_op | source)
XLA Modules:
  0.0 85.2 jit_solution(59282007581467633)
XLA Ops:
  0.6 82.8 %shard_map.68 = (f32[4,128]{1,0:T(4,128)}, f32[1,128]{1,0:T(1,128)}) custom-call(bf16[512,768]{1,0:T(8,128)(2,1)} %src_in.1, bf16[128,768]{1,0:T(8,128)(2,1)} %tgt_in.1, f32[1,128]{1,0:T(1,128)} %bitcast.7, f32[4,128]{1,0:T(4,128)} %bitcast.5, f32[1,128]{1,0:T(1,128)} %bitcast.8), custom_call_target="tpu_custom_call" | custom-call | tf_op jit(solution)/shard_map/pallas_call | solution.py:456
  83.4 0.0 copy-start
  83.4 0.7 copy-done
  84.1 0.0 copy-start.1
  84.1 0.6 copy.9
  84.6 0.1 copy-done.1
  84.7 0.5 copy.10
Async XLA Ops:
  83.4 0.7 copy-start
  84.1 0.6 copy-start.1

commit v5 on v4

--- a/solution.py
+++ b/solution.py
@@ -28,7 +28,7 @@
 def kernel(
     src_in, tgt_in, init_in, slogw_in, tlogw_in, row_out, col_out,
     src, buf_a, buf_b, aux, cost, grep, gsend, gbuf, mrow, srow, frep, wrow, lrow, lget, frow,
-    ltile, lsend, abuf, zsend, bbuf, fbuf, hbuf,
+    ctop, csum, ltile, lsend, abuf, zsend, bbuf, fbuf, hbuf,
     send, recv, loc, token,
 ):
     b, g = lax.axis_index("blk"), lax.axis_index("grp")
@@ -261,16 +261,15 @@
                     tile = jnp.where(chunk == pv, w, tile)
                 grep[8 + zp * 2 + k] = jnp.broadcast_to(tile, (8, 128))
 
-    def row_tiles(tiles, more=False):
-        @pl.loop(0, 256, unroll=8)
+    halves = [lax.rem(x + k, 2) for k in range(2)]
+
+    def row_pass(hd):
+        @pl.loop(0, 128, unroll=8)
         def _(i):
-            r = pl.ds(pl.multiple_of(i * 8, 8), 8)
+            r = pl.ds(pl.multiple_of(1024 * hd + i * 8, 8), 8)
             top = total = None
-            tl = list(tiles)
-            if more:
-                top, total = mrow[r, :], srow[r, :]
-            for c in range(0, len(tl), 8):
-                stack = jnp.stack([cost[t, r, :] + grep[t] for t in tl[c : c + 8]])
+            for c in range(0, 16, 8):
+                stack = jnp.stack([cost[t, r, :] + grep[t] for t in range(c, c + 8)])
                 new = jnp.max(stack, axis=0)
                 if top is not None:
                     new = jnp.maximum(top, new)
@@ -280,36 +279,61 @@
             mrow[r, :] = top
             srow[r, :] = total
 
-    def row_lse():
-        for q in range(16):
-            r = slice(128 * q, 128 * q + 128)
-            m = mrow[r, :].T
-            top = jnp.max(m, axis=0, keepdims=True)
-            total = jnp.sum(srow[r, :].T * jnp.exp2(m - top), axis=0, keepdims=True)
-            lrow[q // 4, q % 4 : q % 4 + 1, :] = top + jnp.log2(total)
-
-    def row_swap(it):
-        swaps = [remote(lrow, lget.at[it, k], mates[k]) for k in range(3)]
-        for copy in swaps:
+        for k in range(2):
+            for q in range(4):
+                r = pl.ds(pl.multiple_of(1024 * hd + 512 * k + 128 * q, 128), 128)
+                m = mrow[r, :].T
+                top = jnp.max(m, axis=0, keepdims=True)
+                total = jnp.sum(srow[r, :].T * jnp.exp2(m - top), axis=0, keepdims=True)
+                lrow[2 * hd + k, q : q + 1, :] = top + jnp.log2(total)
+
+    def swap_rows(it, hd):
+        swaps = []
+        for k in range(3):
+            theirs = hd if k == 0 else 1 - hd
+            mine = pl.ds(2 * hd, 2)
+            copy = remote(lrow.at[mine], lget.at[it, k, mine], mates[k])
             copy.start()
-        for copy in swaps:
-            copy.wait_recv()
+            other = lget.at[it, k, pl.ds(2 * theirs, 2)]
+            swaps.append((copy, remote(other, other, mates[k], count[0] - 1)))
+        return swaps
+
+    def finish_rows(it, hd, swaps):
+        for copy, arrival in swaps:
+            arrival.wait_recv()
             copy.wait_send()
-        for slot in range(4):
-            terms = [lrow[slot]] + [lget[it, k, slot ^ (k + 1)] for k in range(3)]
+        for k in range(2):
+            slot = 2 * hd + k
+            terms = [
+                lrow[slot], lget[it, 0, 2 * hd + 1 - k], lget[it, 1, 2 * (1 - hd) + k], lget[it, 2, 2 * (1 - hd) + 1 - k],
+            ]
             frow[slot] = LOG2E * wrow[slot] - lse2(jnp.stack(terms))
-        for q in range(16):
-            line_ = jnp.broadcast_to(frow[q // 4, q % 4 : q % 4 + 1, :], (128, 128))
-            col = jnp.sum(jnp.where(eye, line_, 0.0), axis=1, keepdims=True)
-            frep[128 * q : 128 * q + 128, :] = jnp.broadcast_to(col, (128, 128))
+            for q in range(4):
+                r = pl.ds(pl.multiple_of(1024 * hd + 512 * k + 128 * q, 128), 128)
+                line_ = jnp.broadcast_to(frow[slot, q : q + 1, :], (128, 128))
+                col = jnp.sum(jnp.where(eye, line_, 0.0), axis=1, keepdims=True)
+                frep[r, :] = jnp.broadcast_to(col, (128, 128))
+
+    def sweep(it):
+        row_pass(halves[0])
+        early = swap_rows(it, halves[0])
+        row_pass(halves[1])
+        late = swap_rows(it, halves[1])
+        finish_rows(it, halves[0], early)
+
+        @pl.loop(0, 16, unroll=2)
+        def _(t):
+            ctop[t], csum[t] = col_half(t, halves[0], None, None)
+
+        finish_rows(it, halves[1], late)
+        return col_reduce(it)
 
     def offset(place):
         return jnp.where(place == 0, 0, jnp.where(place == 1, 3, jnp.where(place == 2, 1, 2)))
 
-    def col_tile(tile):
-        top = total = None
-        for q in range(16):
-            r = slice(128 * q, 128 * q + 128)
+    def col_half(tile, hd, top, total):
+        for q in range(8):
+            r = pl.ds(pl.multiple_of(1024 * hd + 128 * q, 128), 128)
             w = (cost[tile, r, :] + frep[r, :]).reshape(16, 8, 128)
             new = jnp.max(w, axis=0)
             if top is not None:
@@ -317,6 +341,10 @@
             part = jnp.sum(jnp.exp2(w - new[None]), axis=0)
             total = part if top is None else total * jnp.exp2(top - new) + part
             top = new
+        return top, total
+
+    def col_tile(tile):
+        top, total = col_half(tile, halves[1], ctop[tile], csum[tile])
         peak = jnp.max(top, axis=0, keepdims=True)
         mass = jnp.sum(total * jnp.exp2(top - peak), axis=0, keepdims=True)
         return peak + jnp.log2(mass)
@@ -332,7 +360,7 @@
         def group(i):
             return (1 - lax.rem(i, 2)) * 4 + 3 - lax.div(i, 2)
 
-        @pl.loop(0, 8)
+        @pl.loop(0, 8, unroll=2)
         def _(i):
             ltile[i] = col_tile(8 + i)
 
@@ -381,17 +409,18 @@
         multiply_b(n, 3)
 
     spread()
-    row_tiles(range(16))
-    row_lse()
-    row_swap(0)
-    zsend[0] = col_reduce(0)
+    zsend[0] = sweep(0)
     pl.semaphore_wait(token, 2)
+    sent = list(started)
+    started.clear()
     waits = []
     for dz, peer in line:
         copy = remote(zsend.at[0], bbuf.at[dz], peer)
         go(copy)
         waits.append(copy)
     bbuf[0] = zsend[0]
+    for copy in sent:
+        copy.wait_send()
     for copy in waits:
         copy.wait_recv()
     gsend[...] = own_w - lse2(bbuf[...])
@@ -408,11 +437,7 @@
         remote(gbuf.at[there], gbuf.at[there], partner, slot).wait_recv()
 
     spread()
-    row_tiles(range(16))
-    row_lse()
-    row_swap(1)
-    row_out[...] = frow[0] * (1.0 / TO2)
-    zsend[1] = col_reduce(1)
+    zsend[1] = sweep(1)
     waits = []
     for dz, peer in line:
         copy = remote(zsend.at[1], fbuf.at[0, dz], peer)
@@ -423,6 +448,7 @@
         go(copy)
         waits.append(copy)
     fbuf[0, 0] = zsend[1]
+    row_out[...] = frow[0] * (1.0 / TO2)
     for copy in waits:
         copy.wait_recv()
     hbuf[core] = lse2(fbuf[0])
@@ -446,7 +472,7 @@
         copy.wait_send()
 
 
-N_SEM = 66 + 9 + 12 + 6 + 16 + 7 + 7 + 15
+N_SEM = 66 + 9 + 12 + 12 + 16 + 7 + 7 + 15
 
 
 def shards(source_embed, target_embed, target_init, source_logw, target_logw):
@@ -474,6 +500,8 @@
             pltpu.VMEM((4, 4, 128), f32),
             pltpu.VMEM((2, 3, 4, 4, 128), f32),
             pltpu.VMEM((4, 4, 128), f32),
+            pltpu.VMEM((16, 8, 128), f32),
+            pltpu.VMEM((16, 8, 128), f32),
             pltpu.VMEM((8, 1, 128), f32),
             pltpu.VMEM((8, 2, 128), f32),
             pltpu.VMEM((2, 8, 2, 128), f32),

time: 85.4 us -> 84.7 us (level)
  no operation moved by 1% of the time
where the time goes in v5:
time: 84.7 us; the launch traced here: 84.6 us
  Pallas kernels  82.1 us (97%)
  local copies, waits for them, and re-layouts  1.8 us (2%)
    pallas_call x1, Pallas kernels, shards(): pl.pallas_call(kernel, out_shape=(jax.ShapeDtypeStruct((4, 128), f32), ja...  82.1 us
    unnamed x6, local copies, waits for them, and re-layouts  1.8 us

profile of v5, /device:TPU:1, one launch (start us, length us, event | category | flops | bytes accessed | tf_op | source)
XLA Modules:
  0.0 84.6 jit_solution(9731859757653458491)
XLA Ops:
  0.6 82.1 %shard_map.68 = (f32[4,128]{1,0:T(4,128)}, f32[1,128]{1,0:T(1,128)}) custom-call(bf16[512,768]{1,0:T(8,128)(2,1)} %src_in.1, bf16[128,768]{1,0:T(8,128)(2,1)} %tgt_in.1, f32[1,128]{1,0:T(1,128)} %bitcast.7, f32[4,128]{1,0:T(4,128)} %bitcast.5, f32[1,128]{1,0:T(1,128)} %bitcast.8), custom_call_target="tpu_custom_call" | custom-call | tf_op jit(solution)/shard_map/pallas_call | solution.py:482
  82.8 0.0 copy-start
  82.8 0.7 copy-done
  83.4 0.0 copy-start.1
  83.5 0.6 copy.9
  84.0 0.1 copy-done.1
  84.1 0.5 copy.10
Async XLA Ops:
  82.8 0.7 copy-start
  83.4 0.6 copy-start.1

commit v6 on v5

--- a/solution.py
+++ b/solution.py
@@ -169,8 +169,12 @@
         t.near[0].begin()
     aux_rings[0].mid()
     for t in trees:
+        t.own[0].mid()
+    for t in trees:
         t.two[1].mid()
         t.near[1].begin()
+    for t in trees:
+        t.own[1].mid()
     aux_rings[0].end()
     aux_rings[1].begin()
     for t in trees:
@@ -181,9 +185,6 @@
     for t in trees:
         t.two[1].end()
         t.far[1].begin()
-    for k in range(2):
-        for t in trees:
-            t.own[k].mid()
     aux_rings[1].mid()
     for copy in to_all:
         copy.wait_recv()
@@ -448,7 +449,8 @@
         go(copy)
         waits.append(copy)
     fbuf[0, 0] = zsend[1]
-    row_out[...] = frow[0] * (1.0 / TO2)
+    for q in range(4):
+        row_out[128 * q : 128 * q + 128] = frow[0, q] * (1.0 / TO2)
     for copy in waits:
         copy.wait_recv()
     hbuf[core] = lse2(fbuf[0])
@@ -466,7 +468,7 @@
             )
             out = jnp.where(zl == k, w, out)
         total = jnp.where(lax.div(lanes, 64) == c, out, total)
-    col_out[...] = 0.1 * tlogw_in[...] - (1.0 / TO2) * total
+    col_out[...] = (0.1 * tlogw_in[...] - (1.0 / TO2) * total)[0]
 
     for copy in started:
         copy.wait_send()
@@ -481,7 +483,7 @@
     hbm = pl.BlockSpec(memory_space=pl.ANY)
     row, col = pl.pallas_call(
         kernel,
-        out_shape=(jax.ShapeDtypeStruct((4, 128), f32), jax.ShapeDtypeStruct((1, 128), f32)),
+        out_shape=(jax.ShapeDtypeStruct((512,), f32), jax.ShapeDtypeStruct((128,), f32)),
         in_specs=[hbm, hbm, vmem, vmem, vmem],
         out_specs=(vmem, vmem),
         scratch_shapes=[
@@ -521,7 +523,7 @@
         source_embed, target_embed, target_init.reshape(1, 128),
         source_logw.reshape(4, 128), target_logw.reshape(1, 128),
     )
-    return row.reshape(512), col.reshape(128)
+    return row, col
 
 
 def solution(mesh):

time: 84.7 us -> 84.7 us (level)
  no operation moved by 1% of the time
where the time goes in v6:
time: 84.7 us; the launch traced here: 84.6 us
  Pallas kernels  82.1 us (97%)
  local copies, waits for them, and re-layouts  1.8 us (2%)
    pallas_call x1, Pallas kernels, shards(): pl.pallas_call(kernel, out_shape=(jax.ShapeDtypeStruct((512,), f32), jax....  82.1 us
    unnamed x6, local copies, waits for them, and re-layouts  1.8 us

profile of v6, /device:TPU:1, one launch (start us, length us, event | category | flops | bytes accessed | tf_op | source)
XLA Modules:
  0.0 84.6 jit_solution(17774448656494675719)
XLA Ops:
  0.6 82.1 %shard_map.68 = (f32[512]{0:T(512)}, f32[128]{0:T(128)}) custom-call(bf16[512,768]{1,0:T(8,128)(2,1)} %src_in.1, bf16[128,768]{1,0:T(8,128)(2,1)} %tgt_in.1, f32[1,128]{1,0:T(1,128)} %bitcast.4, f32[4,128]{1,0:T(4,128)} %bitcast.3, f32[1,128]{1,0:T(1,128)} %bitcast.5), custom_call_target="tpu_custom_call" | custom-call | tf_op jit(solution)/shard_map/pallas_call | solution.py:484
  82.8 0.0 copy-start
  82.8 0.7 copy-done
  83.4 0.0 copy-start.1
  83.5 0.6 copy.9
  84.0 0.1 copy-done.1
  84.1 0.5 copy.10
Async XLA Ops:
  82.8 0.7 copy-start
  83.4 0.6 copy-start.1
